TPU v7x, 128 devices: a whole 4x4x4 slice. The times are simulated.
128 devices in a mesh: row: 32 (over y, z, core), col: 4 (over x).
Axes of the slice: x: 4, y: 4, z: 4, core: 2. Of those that a mesh axis runs over, the one named last changes fastest.
Arguments:
- amplitudes: bfloat16 [4, 1280, 1280], P(None, ('row', 'col')), may hold values from -0.75 to 0.75
- integrals: bfloat16 [96, 1280, 1280], P('row', 'col'), may hold values from -0.15625 to 0.15625
- occupied_integrals: bfloat16 [96, 160, 1280], P('row'), may hold values from -1 to 1
- pair_orbitals: int32 [4, 2], replicated, may hold values from 0 to 159
- amplitude_tiles: int32 [4, 20, 20], replicated, may hold values 0 or 1
- integral_tiles: int32 [20, 20], replicated, may hold values 0 or 1
Outputs:
- residual: float32 [4, 1280, 1280], P(None, 'col', 'row')
All inputs are finite; a program needn't handle non-finite values.
Results may differ from a plain program's by a relative error of at most 0.005.
Values may be sent and summed in bfloat16 or wider, within the bound.
A program may use at most 128 MiB of HBM per device.

v0:
```python
import jax
import jax.numpy as jnp
from jax import lax
from jax.sharding import PartitionSpec as P

TILE = 64


def mask_rows(amp_rows, amp_tiles, tile_size):
    row_count = amp_rows.shape[1]
    tile_count = amp_tiles.shape[1]
    tile_of = jnp.arange(row_count, dtype=jnp.int32) // tile_size
    picker = (tile_of[:, None] == jnp.arange(tile_count, dtype=jnp.int32)[None, :]).astype(
        jnp.float32
    )
    row_mask = jnp.einsum("nk,pkm->pnm", picker, amp_tiles.astype(jnp.float32))
    row_mask = jnp.repeat(row_mask, tile_size, axis=2)
    return amp_rows * row_mask.astype(amp_rows.dtype)


def local(
    amplitudes, integrals, occupied_integrals, pair_orbitals, amplitude_tiles, integral_tiles
):
    column_index = lax.axis_index("col")
    local_rows = integrals.shape[1]
    tiles_here = local_rows // TILE
    tile_rows = lax.dynamic_slice_in_dim(integral_tiles, column_index * tiles_here, tiles_here, 0)
    factor_mask = jnp.repeat(jnp.repeat(tile_rows, TILE, axis=0), TILE, axis=1)
    masked_int = integrals * factor_mask.astype(jnp.bfloat16)[None]
    orbital_ids = jnp.arange(occupied_integrals.shape[1], dtype=jnp.int32)
    pick_first = (pair_orbitals[:, 0][:, None] == orbital_ids[None, :]).astype(jnp.bfloat16)
    pick_second = (pair_orbitals[:, 1][:, None] == orbital_ids[None, :]).astype(jnp.bfloat16)
    first_rows = jnp.einsum(
        "po,qov->qpv", pick_first, occupied_integrals, preferred_element_type=jnp.float32
    )
    second_rows = jnp.einsum(
        "po,qov->qpv", pick_second, occupied_integrals, preferred_element_type=jnp.float32
    ).astype(jnp.bfloat16)
    whole_amp = lax.all_gather(amplitudes, ("row", "col"), axis=1, tiled=True)
    masked_amp = mask_rows(whole_amp, amplitude_tiles, TILE)
    inter = jnp.einsum(
        "qac,pcd->qpad", masked_int, masked_amp, preferred_element_type=jnp.float32
    ).astype(jnp.bfloat16)
    carried = jnp.einsum(
        "qpc,pcd->qpd", second_rows, masked_amp, preferred_element_type=jnp.float32
    )
    first_here = lax.dynamic_slice_in_dim(first_rows, column_index * local_rows, local_rows, 2)
    ladder = jnp.einsum(
        "qpad,qbd->pab",
        inter,
        lax.all_gather(masked_int, "col", axis=1, tiled=True),
        preferred_element_type=jnp.float32,
    )
    cycle = jnp.einsum("qpa,qpb->pab", first_here, carried)
    return lax.psum_scatter(ladder + cycle, "row", scatter_dimension=2, tiled=True)


def solution(mesh):
    placed = (
        P(None, ("row", "col"), None),
        P("row", "col", None),
        P("row", None, None),
        P(),
        P(),
        P(),
    )
    return jax.shard_map(
        local, mesh=mesh, in_specs=placed, out_specs=P(None, "col", "row"), check_vma=False
    )
```

profile of v0, /device:TPU:1, one launch (start us, length us, event | category | flops | bytes accessed | tf_op | source)
XLA Modules:
  0.0 316.9 jit_solution(4331648339381374294)
XLA Ops:
  6.5 0.0 copy-start
  6.5 0.0 all-gather.3.cloned.1.call-start
  6.5 0.7 all-gather.3.cloned.1.call-update
  7.3 0.0 all-gather.5.cloned.1.call-start
  7.3 0.7 dynamic-slice_convert_fusion
  8.0 0.1 copy.23
  8.1 0.1 broadcast_in_dim.7
  8.2 0.1 convert_element_type.48
  8.3 0.1 broadcast_in_dim.16
  8.4 0.6 copy.24
  9.0 3.4 %broadcast_multiply_fusion = bf16[3,320,1280]{2,1,0:T(8,128)(2,1)} fusion(bf16[3,320,1280]{2,1,0:T(8,128)(2,1)} %param.7, bf16[320,1280]{1,0:T(8,128)(2,1)S(1)} %copy.24), kind=kLoop, calls=%fused_computation.13 | loop fusion | flops 1228800 | bytes 5734400 | tf_op jit(solution)/shard_map/mul | solution.py:29
  12.5 0.0 all-gather.5.cloned.1.call-update
  12.5 0.0 reduce-scatter.2.cloned.1.call-start
  12.6 0.0 copy-done.4
  12.6 0.0 copy-done.5
  12.6 0.0 copy-done
  12.6 0.3 fusion.20
  12.9 0.1 dynamic-slice_bitcast_fusion
  13.0 0.3 fusion.7
  13.3 0.3 fusion.8
  13.6 74.5 %all-gather.3.cloned.1.call-done = bf16[4,1280,1280]{2,0,1:T(4,128)(2,1)} async-done(((bf16[4,10,1280]{2,0,1:T(4,128)(2,1)}), bf16[4,1280,1280]{2,0,1:T(4,128)(2,1)}) %all-gather.3.cloned.1.call-update) | async-done | bytes 13107216 | tf_op jit(solution)/shard_map/all_gather | solution.py:39
  88.1 21.2 %copy.22 = bf16[4,1280,1280]{1,2,0:T(8,128)(2,1)} copy(bf16[4,1280,1280]{2,0,1:T(4,128)(2,1)} %all-gather.3.cloned.1.call-done) | data formatting | bytes 26214400 | tf_op jit(solution)/shard_map/all_gather | solution.py:39
  109.4 6.4 %bitcast_multiply_fusion = bf16[4,1280,1280]{1,2,0:T(8,128)(2,1)S(1)} fusion(bf16[4,1280,1280]{1,2,0:T(8,128)(2,1)} %copy.22, bf16[4,1280,20]{1,2,0:T(8,128)(2,1)S(1)} %fusion.7), kind=kLoop, calls=%fused_computation.2 | loop fusion | flops 6553600 | bytes 26419200 | tf_op jit(solution)/shard_map/mul | solution.py:18
  115.8 0.0 copy-start.2
  115.8 4.7 %copy-done.2 = bf16[4,1280,1280]{1,2,0:T(8,128)(2,1)} copy-done((bf16[4,1280,1280]{1,2,0:T(8,128)(2,1)}, bf16[4,1280,1280]{1,2,0:T(8,128)(2,1)S(1)}, u32[]{:S(2)}) %copy-start.2) | copy-done | bytes 13107224
  120.5 0.0 copy-done.3
  120.5 15.0 %fusion.1 = bf16[3,4,320,1280]{3,2,0,1:T(8,128)(2,1)} fusion(bf16[4,1280,1280]{1,2,0:T(8,128)(2,1)S(1)} %bitcast_multiply_fusion, bf16[3,320,1280]{2,1,0:T(8,128)(2,1)S(1)} %copy-done.3), kind=kOutput, calls=%fused_computation.3 | convolution fusion | flops 12587827200 | bytes 25395200 | tf_op jit(solution)/shard_map/qac,pcd->qpad/dot_general | solution.py:41
  135.4 48.5 %all-gather.5.cloned.1.call-done = bf16[3,1280,1280]{2,1,0:T(8,128)(2,1)} async-done(((bf16[3,320,1280]{2,1,0:T(8,128)(2,1)}), bf16[3,1280,1280]{2,1,0:T(8,128)(2,1)}) %all-gather.5.cloned.1.call-update) | async-done | bytes 9830416 | tf_op jit(solution)/shard_map/all_gather | solution.py:51
  184.0 21.9 %fusion.4 = f32[4,320,1280,1]{1,2,3,0:T(8,128)} fusion(bf16[3,4,320,1280]{3,2,0,1:T(8,128)(2,1)} %fusion.1, bf16[3,1280,1280]{2,1,0:T(8,128)(2,1)} %all-gather.5.cloned.1.call-done), kind=kOutput, calls=%fused_computation.4 | convolution fusion | flops 12582912000 | bytes 26214400 | tf_op jit(solution)/shard_map/qpad,qbd->pab/dot_general | solution.py:48
  205.8 14.8 %bitcast_add_fusion = f32[4,320,1280]{1,2,0:T(8,128)} fusion(f32[4,320,1280,1]{1,2,3,0:T(8,128)} %fusion.4, bf16[4,1280,1280]{1,2,0:T(8,128)(2,1)} %copy-done.2, bf16[3,4,1280]{2,1,0:T(4,128)(2,1)S(1)} %fusion.8, bf16[3,4,320]{2,1,0:T(4,128)(2,1)S(1)} %dynamic-slice_bitcast_fusion), kind=kOutput, calls=%fused_computation.6 | convolution fusion | flops 50790400 | bytes 26252800 | tf_op jit(solution)/shard_map/qpa,qpb->pab/dot_general | solution.py:54
  220.6 0.0 reduce-scatter.2.cloned.1.call-update
  220.7 89.7 %reduce-scatter.2.cloned.1.call-done = f32[4,320,40]{1,2,0:T(8,128)} async-done(((f32[4,320,1280]{1,2,0:T(8,128)}), f32[4,320,40]{1,2,0:T(8,128)}) %reduce-scatter.2.cloned.1.call-update) | async-done | bytes 204816 | tf_op jit(solution)/shard_map/reduce_scatter | solution.py:55
  (8 shorter events, 0.0 us)
Async XLA Ops:
  6.5 6.1 %copy-start = (bf16[3,160,1280]{2,1,0:T(8,128)(2,1)S(1)}, bf16[3,160,1280]{2,1,0:T(8,128)(2,1)}, u32[]{:S(2)}) copy-start(bf16[3,160,1280]{2,1,0:T(8,128)(2,1)} %param.8) | copy-start | bytes 3686404
  6.5 6.0 %copy-start.4 = (s32[4,20,20]{2,0,1:T(4,128)S(1)}, s32[4,20,20]{2,0,1:T(4,128)}, u32[]{:S(2)}) copy-start(s32[4,20,20]{2,0,1:T(4,128)} %param.10) | copy-start | bytes 19204
  6.5 6.1 %copy-start.5 = (s32[4,2]{0,1:T(2,128)S(1)}, s32[4,2]{0,1:T(2,128)}, u32[]{:S(2)}) copy-start(s32[4,2]{0,1:T(2,128)} %param.9) | copy-start | bytes 100
  6.5 81.6 %all-gather.3.cloned.1.call-start = ((), (), s32[]{:S(2)}) async-start(), calls=%async_computation.1 | async-start | bytes 13209600 | tf_op jit(solution)/shard_map/all_gather | solution.py:39
  7.3 176.7 %all-gather.5.cloned.1.call-start = ((), (), s32[]{:S(2)}) async-start(), calls=%async_computation.2 | async-start | bytes 12288000 | tf_op jit(solution)/shard_map/all_gather | solution.py:51
  12.5 297.9 %reduce-scatter.2.cloned.1.call-start = ((), (), s32[]{:S(2)}) async-start(), calls=%async_computation.3 | async-start | bytes 8110080 | tf_op jit(solution)/shard_map/reduce_scatter | solution.py:55
  109.4 11.1 %copy-start.3 = (bf16[3,320,1280]{2,1,0:T(8,128)(2,1)S(1)}, bf16[3,320,1280]{2,1,0:T(8,128)(2,1)}, u32[]{:S(2)}) copy-start(bf16[3,320,1280]{2,1,0:T(8,128)(2,1)} %broadcast_multiply_fusion) | copy-start | bytes 7372804
  115.8 4.7 %copy-start.2 = (bf16[4,1280,1280]{1,2,0:T(8,128)(2,1)}, bf16[4,1280,1280]{1,2,0:T(8,128)(2,1)S(1)}, u32[]{:S(2)}) copy-start(bf16[4,1280,1280]{1,2,0:T(8,128)(2,1)S(1)} %bitcast_multiply_fusion) | copy-start | bytes 39321604
  205.8 104.6 %copy-start.1 = (bf16[3,160,1280]{2,1,0:T(8,128)(2,1)S(1)}, bf16[3,160,1280]{2,1,0:T(8,128)(2,1)}, u32[]{:S(2)}) copy-start(bf16[3,160,1280]{2,1,0:T(8,128)(2,1)} %param.8) | copy-start | bytes 3686404
Sparse Core Ops, SparseCore 0:
  10.3 77.7 all-gather.2
  89.8 94.1 all-gather.4
  220.8 89.5 reduce-scatter.1
where the time goes:
time: 319 us; the launch traced here: 317 us
  waiting for transfers between devices  213 us (67%)
  matrix products  52.5 us (16%)
  local copies, waits for them, and re-layouts  27 us (8%)
  between operations  13.2 us (4%)
  other arithmetic  10.6 us (3%)
    reduce_scatter x1, waiting for transfers between devices, local(): lax.psum_scatter(ladder + cycle, 'row', scatter_dimension=2, tiled=True)  89.7 us
    all_gather x1, waiting for transfers between devices, local(): whole_amp = lax.all_gather(amplitudes, ('row', 'col'), axis=1, tiled=True)  74.5 us
    all_gather x1, waiting for transfers between devices, local(): lax.all_gather(masked_int, 'col', axis=1, tiled=True)  48.5 us
    dot_general x1, matrix products, local(): jnp.einsum('qpad,qbd->pab', inter, lax.all_gather(masked_int, 'col', axis...  21.9 us
    all_gather x1, local copies, waits for them, and re-layouts, local(): whole_amp = lax.all_gather(amplitudes, ('row', 'col'), axis=1, tiled=True)  21.2 us
    dot_general x1, matrix products, local(): jnp.einsum('qac,pcd->qpad', masked_int, masked_amp, preferred_element_typ...  15 us
    dot_general x1, matrix products, local(): cycle = jnp.einsum('qpa,qpb->pab', first_here, carried)  14.8 us
    mul x1, other arithmetic, mask_rows(): return amp_rows * row_mask.astype(amp_rows.dtype)  6.39 us
  transfers between devices with their start and end apart: 3, of which 3 were waited for; matrix products, arithmetic and copies ran while one was open for 15% of the time, Pallas kernels for 0%

commit v1 on v0

v1 whole, which is shorter than its diff:
```python
import jax
import jax.numpy as jnp
from jax import lax
from jax.experimental import pallas as pl
from jax.experimental.pallas import tpu as pltpu
from jax.sharding import PartitionSpec as P

MESH = pl.DeviceIdType.MESH
TILE = 64
V = 1280
BLK = 320
PIECE = 80
HALF = 640
NT = 256
NS = 2
SUB = BLK // NS
F32 = jnp.float32
BF16 = jnp.bfloat16


def kernel(
    b_own, t_own, l_own, out,
    bbuf, tst, tbuf, lbuf, ut, li2, xbuf, acc,
    s1, r1, s2, r2, fin, gbuf, hbuf,
    t1_ss, t1_rs, tg_ss, tg_rs, l_ss, l_rs, own_ls,
    bo_ss, bf_ss, b_rs, sh_ss, sh_rs, p1_ss, p1_rs, p2_ss, p2_rs, g_ss, g_rs,
):
    x = lax.axis_index("col")
    row = lax.axis_index("row")
    k = lax.rem(row, 2)
    yz = row // 2
    y = yz // 4
    z = lax.rem(yz, 4)
    s = 1 - 2 * lax.rem(x, 2)
    xp = lax.rem(x + s + 4, 4)
    xm = lax.rem(x - s + 4, 4)
    xo = lax.rem(x + 2, 4)
    sg = 1 - 2 * k
    me8 = k * 4 + x
    pair = 2 * lax.rem(x, 2) + k
    sib = (yz * 2 + 1 - k, x)
    owner2 = lax.rem((x + 1) // 2 + 1, 2)
    is_owner = k == owner2
    main_j = x // 2

    def dev(yy, zz, kk, xx):
        return ((yy * 4 + zz) * 2 + kk, xx)

    def ring(v):
        return lax.rem(v + 8, 4)

    def peer8(d):
        idx = lax.rem(me8 + d, 8)
        return idx, idx // 4, lax.rem(idx, 4)

    def rcopy(src, dst, ss, rs, to):
        return pltpu.make_async_remote_copy(
            src_ref=src, dst_ref=dst, send_sem=ss, recv_sem=rs, device_id=to, device_id_type=MESH
        )

    pending = []

    def send(src, dst, ss, rs, to):
        c = rcopy(src, dst, ss, rs, to)
        c.start()
        pending.append(c)
        return c

    barrier = pltpu.get_barrier_semaphore()
    for d in range(1, 8):
        _, kk, xx = peer8(d)
        pl.semaphore_signal(barrier, inc=1, device_id=dev(y, z, kk, xx), device_id_type=MESH)
    for step in (1, -1):
        pl.semaphore_signal(barrier, inc=1, device_id=dev(ring(y + step), z, k, x), device_id_type=MESH)
        pl.semaphore_signal(barrier, inc=1, device_id=dev(y, ring(z + step), k, x), device_id_type=MESH)
    pl.semaphore_wait(barrier, 11)

    for d in range(1, 8):
        idx, kk, xx = peer8(d)
        send(t_own.at[2 * lax.rem(xx, 2) + kk], tst.at[me8], t1_ss.at[d], t1_rs.at[d], dev(y, z, kk, xx))
    send(l_own.at[2 * lax.rem(x, 2) + 1 - k], lbuf.at[1], l_ss, l_rs, sib)

    dest2 = jnp.where(is_owner, xm, xp)
    which2 = jnp.where(is_owner, 0, 2)

    def rows(i):
        return pl.ds(i * SUB, SUB)

    for i in range(NS):
        send(b_own.at[1 - main_j, rows(i)], bbuf.at[k, x, rows(i)], bo_ss.at[1, i], b_rs.at[0, 2, i],
             (row, xm))
        send(b_own.at[main_j, rows(i)], bbuf.at[k, x, rows(i)], bo_ss.at[0, i], b_rs.at[0, 0, i],
             (row, xp))
    for i in range(NS):
        send(b_own.at[2, rows(i)], bbuf.at[2, x, rows(i)], bo_ss.at[2, i], b_rs.at[1, which2, i],
             (row, dest2))

    def share(kind, pos, i, src=None):
        slot, blk = (k, None) if kind == 0 else (2, None)
        blk = (x, pos_main(pos) if kind == 0 else pos_second(pos))[pos > 0]
        dst = bbuf.at[slot, blk, rows(i)]
        return rcopy(dst if src is None else src, dst, sh_ss.at[kind, pos, i], sh_rs.at[kind, pos, i], sib)

    def pos_main(pos):
        return (x, xm, xp, xo)[pos]

    def pos_second(pos):
        return (x, xp, xm, xo)[pos]

    which_of = (None, 2, 0, 1)

    for i in range(NS):
        c = share(0, 0, i, b_own.at[main_j, rows(i)])
        c.start()
        pending.append(c)

    @pl.when(is_owner)
    def _():
        for i in range(NS):
            share(1, 0, i, b_own.at[2, rows(i)]).start()

    own_main = pltpu.make_async_copy(b_own.at[main_j], bbuf.at[k, x], own_ls.at[0])
    own_main.start()
    own_second = pltpu.make_async_copy(b_own.at[2], bbuf.at[2, x], own_ls.at[1])

    @pl.when(is_owner)
    def _():
        own_second.start()

    tst[me8] = t_own[pair]
    lbuf[0] = l_own[pair]
    for d in range(1, 8):
        src8 = lax.rem(me8 + 8 - d, 8)
        rcopy(t_own.at[0], tst.at[src8], t1_ss.at[d], t1_rs.at[d], sib).wait_recv()
    ri = lax.broadcasted_iota(jnp.int32, (PIECE, 128), 0)
    ci = lax.broadcasted_iota(jnp.int32, (PIECE, 128), 1)
    within = jnp.bitwise_and(ci, 15)
    pick = jnp.where((within < 10) & (ri == jnp.right_shift(ci, 4) * 10 + within), 1.0, 0.0).astype(BF16)
    for n in range(V // NT):
        cols = pl.ds(n * NT, NT)
        piece = jnp.dot(pick, tst[:, :, cols].reshape(128, NT), preferred_element_type=F32)
        tbuf[y, z, :, cols] = piece.astype(BF16)

    col_a, col_b = pl.ds(0, HALF), pl.ds(HALF, HALF)

    def t_slice(half, phase, i):
        if half == 0:
            return tbuf.at[i, z, :, col_a] if phase == 0 else tbuf.at[:, i, :, col_a]
        return tbuf.at[y, i, :, col_b] if phase == 0 else tbuf.at[i, :, :, col_b]

    def along(half, phase, off):
        if (half == 0) == (phase == 0):
            return ring(y + off), dev(ring(y + off), z, k, x)
        return ring(z + off), dev(y, ring(z + off), k, x)

    def t_start(half, phase):
        mine = t_slice(half, phase, along(half, phase, 0)[0])
        for n, off in ((0, sg), (1, -sg)):
            send(mine, mine, tg_ss.at[half, phase, n], tg_rs.at[half, phase, n], along(half, phase, off)[1])

    def t_forward(half, phase):
        got = t_slice(half, phase, along(half, phase, -sg)[0])
        rcopy(got, got, tg_ss.at[half, phase, 0], tg_rs.at[half, phase, 0], sib).wait_recv()
        send(got, got, tg_ss.at[half, phase, 2], tg_rs.at[half, phase, 2], along(half, phase, sg)[1])

    def t_finish(half, phase):
        for n, off in ((1, sg), (2, 2)):
            got = t_slice(half, phase, along(half, phase, off)[0])
            rcopy(got, got, tg_ss.at[half, phase, n], tg_rs.at[half, phase, n], sib).wait_recv()

    for phase in range(2):
        for half in range(2):
            if phase == 1:
                t_finish(half, 0)
            t_start(half, phase)
        for half in range(2):
            t_forward(half, phase)

    def land(kind, pos):
        slot = k if kind == 0 else 2
        blk = pos_main(pos) if kind == 0 else pos_second(pos)
        for i in range(NS):
            ref = bbuf.at[slot, blk, rows(i)]
            rcopy(ref, ref, bo_ss.at[0, i], b_rs.at[kind, which_of[pos], i], sib).wait_recv()
            if pos == 1:
                to = xp if kind == 0 else xm
                rcopy(ref, ref, bf_ss.at[kind, i], b_rs.at[kind, 1, i], (row, to)).start()
            share(kind, pos, i).start()

    def from_sib(kind, pos):
        slot = 1 - k if kind == 0 else 2
        blk = pos_main(pos) if kind == 0 else pos_second(pos)
        for i in range(NS):
            ref = bbuf.at[slot, blk, rows(i)]
            rcopy(ref, ref, sh_ss.at[kind, pos, i], sh_rs.at[kind, pos, i], sib).wait_recv()

    def get_second(pos):
        @pl.when(is_owner)
        def _():
            if pos == 0:
                own_second.wait()
            else:
                land(1, pos)

        @pl.when(jnp.logical_not(is_owner))
        def _():
            from_sib(1, pos)

    def first_product(slot, blk):
        @pl.loop(0, V // NT)
        def _(n):
            cols = pl.ds(pl.multiple_of(n * NT, NT), NT)
            rhs = tbuf[:, :, :, cols].reshape(V, NT)
            val = jnp.dot(bbuf[slot, blk], rhs, preferred_element_type=F32)
            xbuf[slot, pl.ds(pl.multiple_of(blk * BLK, 64), BLK), cols] = val.astype(BF16)

    land(0, 1)
    own_main.wait()
    t_finish(0, 1)
    t_finish(1, 1)
    land(0, 2)
    first_product(k, x)

    rcopy(l_own.at[0], lbuf.at[1], l_ss, l_rs, sib).wait_recv()
    pick_l = jnp.where(k == x // 2, 0, 1)
    for n in range(V // NT):
        cols = pl.ds(n * NT, NT)
        u = jnp.dot(lbuf[pick_l, 0:16], tbuf[:, :, :, cols].reshape(V, NT), preferred_element_type=F32)
        hi = u.astype(BF16).astype(F32)
        both = jnp.concatenate([hi, u - hi], axis=0)
        ut[cols, :] = both.T.astype(BF16)
    li2[0:16] = lbuf[pick_l, 16:32]
    li2[16:32] = lbuf[pick_l, 16:32]

    from_sib(0, 0)
    first_product(1 - k, x)
    get_second(0)
    first_product(2, x)
    get_second(1)
    first_product(k, xm)
    first_product(k, xp)
    from_sib(0, 1)
    first_product(1 - k, xm)
    from_sib(0, 2)
    first_product(1 - k, xp)
    land(0, 3)
    first_product(k, xo)
    get_second(2)
    from_sib(0, 3)
    first_product(1 - k, xo)

    nt = (((1,), (1,)), ((), ()))

    @pl.loop(0, 4)
    def _(m):
        @pl.loop(0, V // NT)
        def _(n):
            cols = pl.ds(pl.multiple_of(n * NT, NT), NT)
            val = jnp.dot(ut[pl.ds(pl.multiple_of(m * BLK, 64), BLK), :], li2[:, cols],
                          preferred_element_type=F32)
            for sl in range(2):
                val += lax.dot_general(bbuf[sl, m], xbuf[sl, cols, :], nt, preferred_element_type=F32)
            acc[m, :, :, cols] = val.reshape(4, PIECE, NT)

    first_product(2, xp)
    first_product(2, xm)
    get_second(3)
    first_product(2, xo)

    def last_product(lo, hi):
        @pl.loop(lo, hi)
        def _(n):
            cols = pl.ds(pl.multiple_of(n * NT, NT), NT)

            @pl.loop(0, 4)
            def _(m):
                val = lax.dot_general(bbuf[2, m], xbuf[2, cols, :], nt, preferred_element_type=F32)
                acc[m, :, :, cols] += val.reshape(4, PIECE, NT)

    def ralong(half, phase, off):
        return along(1 - half, phase, off)

    def part(half, t, i):
        cols = (col_a, col_b)[half]
        return acc[t, i, :, cols] if half == 0 else acc[i, t, :, cols]

    def put(half, t, i, val):
        cols = (col_a, col_b)[half]
        if half == 0:
            acc[t, i, :, cols] = val
        else:
            acc[i, t, :, cols] = val

    def p1_start(half):
        far = ralong(half, 0, 2)[0]
        back, back_dev = ralong(half, 0, -sg)
        fwd_dev = ralong(half, 0, sg)[1]
        for t in range(4):
            s1[half, 0, t] = part(half, t, far).astype(BF16)
        send(s1.at[half, 0], r1.at[half, 0], p1_ss.at[half, 0], p1_rs.at[half, 0], fwd_dev)
        for t in range(4):
            s1[half, 1, t] = part(half, t, back).astype(BF16)
        send(s1.at[half, 1], r1.at[half, 1], p1_ss.at[half, 1], p1_rs.at[half, 1], back_dev)

    def p1_wait(half, n):
        rcopy(s1.at[half, n], r1.at[half, n], p1_ss.at[half, n], p1_rs.at[half, n], sib).wait_recv()

    def p1_middle(half):
        nxt, nxt_dev = ralong(half, 0, sg)
        p1_wait(half, 0)
        for t in range(4):
            s1[half, 2, t] = (part(half, t, nxt) + r1[half, 0, t].astype(F32)).astype(BF16)
        send(s1.at[half, 2], r1.at[half, 2], p1_ss.at[half, 2], p1_rs.at[half, 2], nxt_dev)

    def p1_end(half):
        here = ralong(half, 0, 0)[0]
        p1_wait(half, 1)
        p1_wait(half, 2)

        def total(t):
            return part(half, t, here) + r1[half, 1, t].astype(F32) + r1[half, 2, t].astype(F32)

        far = ralong(half, 1, 2)[0]
        back, back_dev = ralong(half, 1, -sg)
        nxt, nxt_dev = ralong(half, 1, sg)
        s2[half, 0] = total(far).astype(BF16)
        send(s2.at[half, 0], r2.at[half, 0], p2_ss.at[half, 0], p2_rs.at[half, 0], nxt_dev)
        s2[half, 1] = total(back).astype(BF16)
        send(s2.at[half, 1], r2.at[half, 1], p2_ss.at[half, 1], p2_rs.at[half, 1], back_dev)
        put(half, nxt, here, total(nxt))
        mid = ralong(half, 1, 0)[0]
        put(half, mid, here, total(mid))

    def p2_wait(half, n):
        rcopy(s2.at[half, n], r2.at[half, n], p2_ss.at[half, n], p2_rs.at[half, n], sib).wait_recv()

    def p2_middle(half):
        nxt, nxt_dev = ralong(half, 1, sg)
        here = ralong(half, 0, 0)[0]
        p2_wait(half, 0)
        s2[half, 2] = (part(half, nxt, here) + r2[half, 0].astype(F32)).astype(BF16)
        send(s2.at[half, 2], r2.at[half, 2], p2_ss.at[half, 2], p2_rs.at[half, 2], nxt_dev)

    def p2_end(half):
        mid = ralong(half, 1, 0)[0]
        here = ralong(half, 0, 0)[0]
        p2_wait(half, 1)
        p2_wait(half, 2)
        fin[:, (col_a, col_b)[half]] = (
            part(half, mid, here) + r2[half, 1].astype(F32) + r2[half, 2].astype(F32)
        )

    last_product(0, 3)
    p1_start(0)
    last_product(3, 5)
    p1_start(1)
    for step in (p1_middle, p1_end, p2_middle, p2_end):
        for half in range(2):
            step(half)

    for kk in range(2):
        for xx in range(4):
            gbuf[kk * 4 + xx] = fin[kk * 40:(kk + 1) * 40, xx * BLK:(xx + 1) * BLK]
    for d in range(1, 8):
        idx, kk, xx = peer8(d)
        send(gbuf.at[idx], hbuf.at[me8], g_ss.at[d], g_rs.at[d], dev(y, z, kk, xx))
    hbuf[me8] = gbuf[me8]
    for d in range(1, 8):
        src8 = lax.rem(me8 + 8 - d, 8)
        rcopy(gbuf.at[0], hbuf.at[src8], g_ss.at[d], g_rs.at[d], sib).wait_recv()
    for p in range(4):
        src = (p % 2) * 4 + p // 2
        out[p] = hbuf[src] + hbuf[src + 2]

    for c in pending:
        c.wait_send()

    def wait_own(kind, pos_list):
        for pos in pos_list:
            for i in range(NS):
                share(kind, pos, i).wait_send()
        for i in range(NS):
            ref = bbuf.at[k if kind == 0 else 2, xm if kind == 0 else xp, rows(i)]
            rcopy(ref, ref, bf_ss.at[kind, i], b_rs.at[kind, 1, i], (row, xp if kind == 0 else xm)).wait_send()

    wait_own(0, (1, 2, 3))

    @pl.when(is_owner)
    def _():
        wait_own(1, (0, 1, 2, 3))


def exchange(b_own, t_own, l_own):
    vmem = pl.BlockSpec(memory_space=pltpu.VMEM)
    dma = pltpu.SemaphoreType.DMA
    return pl.pallas_call(
        kernel,
        out_shape=jax.ShapeDtypeStruct((4, 40, BLK), F32),
        in_specs=[vmem] * 3,
        out_specs=vmem,
        scratch_shapes=[
            pltpu.VMEM((3, 4, BLK, V), BF16),
            pltpu.VMEM((8, 16, V), BF16),
            pltpu.VMEM((4, 4, PIECE, V), BF16),
            pltpu.VMEM((2, 32, V), BF16),
            pltpu.VMEM((V, 32), BF16),
            pltpu.VMEM((32, V), BF16),
            pltpu.VMEM((3, V, V), BF16),
            pltpu.VMEM((4, 4, PIECE, V), F32),
            pltpu.VMEM((2, 3, 4, PIECE, HALF), BF16),
            pltpu.VMEM((2, 3, 4, PIECE, HALF), BF16),
            pltpu.VMEM((2, 3, PIECE, HALF), BF16),
            pltpu.VMEM((2, 3, PIECE, HALF), BF16),
            pltpu.VMEM((PIECE, V), F32),
            pltpu.VMEM((8, 40, BLK), F32),
            pltpu.VMEM((8, 40, BLK), F32),
            dma((8,)), dma((8,)),
            dma((2, 2, 3)), dma((2, 2, 3)),
            dma, dma,
            dma((2,)),
            dma((3, NS)), dma((2, NS)), dma((2, 3, NS)),
            dma((2, 4, NS)), dma((2, 4, NS)),
            dma((2, 3)), dma((2, 3)), dma((2, 3)), dma((2, 3)),
            dma((8,)), dma((8,)),
        ],
        compiler_params=pltpu.CompilerParams(
            collective_id=0, has_side_effects=True, vmem_limit_bytes=62 * 1024 * 1024
        ),
    )(b_own, t_own, l_own)


def local(
    amplitudes, integrals, occupied_integrals, pair_orbitals, amplitude_tiles, integral_tiles
):
    x = lax.axis_index("col")
    row = lax.axis_index("row")
    tiles_here = BLK // TILE
    tile_rows = lax.dynamic_slice_in_dim(integral_tiles, x * tiles_here, tiles_here, 0)
    factor_mask = jnp.repeat(jnp.repeat(tile_rows, TILE, axis=0), TILE, axis=1)
    masked_int = integrals * factor_mask.astype(BF16)[None]

    amp_rows = amplitudes.shape[1]
    tile_of = ((row * 4 + x) * amp_rows + jnp.arange(amp_rows, dtype=jnp.int32)) // TILE
    picker = (tile_of[:, None] == jnp.arange(V // TILE, dtype=jnp.int32)[None, :]).astype(F32)
    amp_mask = jnp.einsum("nk,pkm->pnm", picker, amplitude_tiles.astype(F32))
    amp_mask = jnp.repeat(amp_mask, TILE, axis=2).astype(BF16)
    masked_amp = jnp.pad(amplitudes * amp_mask, ((0, 0), (0, 16 - amp_rows), (0, 0)))

    orbital_ids = jnp.arange(occupied_integrals.shape[1], dtype=jnp.int32)
    order = pair_orbitals[:, ::-1].reshape(-1)
    pick = (order[:, None] == orbital_ids[None, :]).astype(BF16)
    occ = jnp.einsum("ro,qov->rqv", pick, occupied_integrals, preferred_element_type=F32).astype(BF16)
    occ = jnp.pad(occ, ((0, 0), (0, 13), (0, 0))).reshape(4, 32, V)

    res = exchange(masked_int, masked_amp, occ)
    return jnp.swapaxes(res, 1, 2)


def solution(mesh):
    placed = (
        P(None, ("row", "col"), None),
        P("row", "col", None),
        P("row", None, None),
        P(),
        P(),
        P(),
    )
    return jax.shard_map(
        local, mesh=mesh, in_specs=placed, out_specs=P(None, "col", "row"), check_vma=False
    )
```

time: 319 us -> 134 us (0.42)
  waiting for transfers between devices: 213 us -> 0 us
  Pallas kernels: 0 us -> 123 us
  matrix products: 52.5 us -> 0.51 us
  local copies, waits for them, and re-layouts: 27 us -> 4.73 us
  between operations: 13.2 us -> 0.12 us
  other arithmetic: 10.6 us -> 4.31 us
    pallas_call x0 -> x1, Pallas kernels: none -> 123 us  [exchange(): pl.pallas_call(kernel, out_shape=jax.ShapeDtypeStruct((4, 40, BLK), F32),...]
    all_gather x2 -> x0, waiting for transfers between devices: 123 us -> none  [the longest x1 74.5 us: local(): whole_amp = lax.all_gather(amplitudes, ('row', 'col'), axis=1, tiled=True)]
    reduce_scatter x1 -> x0, waiting for transfers between devices: 89.7 us -> none  [local(): lax.psum_scatter(ladder + cycle, 'row', scatter_dimension=2, tiled=True)]
    dot_general x6 -> x2, matrix products: 52.5 us -> 0.51 us  [the longest x1 0.32 us: local(): jnp.einsum('ro,qov->rqv', pick, occupied_integrals, preferred_element_typ...]
    all_gather x1 -> x0, local copies, waits for them, and re-layouts: 21.2 us -> none  [local(): whole_amp = lax.all_gather(amplitudes, ('row', 'col'), axis=1, tiled=True)]
    mul x2, other arithmetic: 9.84 us -> 3.49 us  [the longest x1 3.43 us: local(): masked_int = integrals * factor_mask.astype(BF16)[None]]
  transfers between devices with their start and end apart: 3 -> 0, of which waited for: 3 -> 0; matrix products, arithmetic and copies ran while one was open for 15% -> 0% of each run, Pallas kernels for 0% -> 0%
where the time goes in v1:
time: 134 us; the launch traced here: 133 us
  Pallas kernels  123 us (92%)
  local copies, waits for them, and re-layouts  4.73 us (4%)
  other arithmetic  4.31 us (3%)
    pallas_call x1, Pallas kernels, exchange(): pl.pallas_call(kernel, out_shape=jax.ShapeDtypeStruct((4, 40, BLK), F32),...  123 us
    mul x1, other arithmetic, local(): masked_int = integrals * factor_mask.astype(BF16)[None]  3.43 us

profile of v1, /device:TPU:1, one launch (start us, length us, event | category | flops | bytes accessed | tf_op | source)
XLA Modules:
  0.0 133.1 jit_solution(4430217481021338894)
XLA Ops:
  0.0 0.0 copy-start
  0.0 0.8 dynamic-slice_convert_fusion
  0.8 0.1 copy.27
  0.9 0.1 broadcast_in_dim.6
  1.0 0.1 convert_element_type.38
  1.1 0.1 broadcast_in_dim.14
  1.2 0.6 copy.28
  1.8 0.0 copy-start.2
  1.8 0.0 copy-start.1
  1.8 0.0 copy-start.3
  1.9 3.4 %broadcast_multiply_fusion.b_own = bf16[3,320,1280]{2,1,0:T(8,128)(2,1)} fusion(bf16[3,320,1280]{2,1,0:T(8,128)(2,1)} %param.7, bf16[320,1280]{1,0:T(8,128)(2,1)S(1)} %copy.28), kind=kLoop, calls=%fused_computation.1 | loop fusion | flops 1228800 | bytes 5734400 | tf_op jit(solution)/shard_map/mul | solution.py:440
  5.3 0.0 copy-done.2
  5.3 0.2 fusion
  5.5 0.2 broadcast_in_dim.15
  5.7 0.2 convert_element_type.43
  5.9 0.0 copy-done.1
  5.9 0.1 mul.25
  6.0 0.7 pad.8.t_own
  6.7 0.0 copy-done.3
  6.7 0.1 copy.32
  6.8 0.1 eq.31
  6.9 0.0 copy-done
  6.9 0.3 convolution_convert_fusion
  7.3 0.7 pad.9.clone
  8.0 123.5 %shard_map.64 = f32[4,40,320]{2,1,0:T(8,128)} custom-call(bf16[3,320,1280]{2,1,0:T(8,128)(2,1)} %broadcast_multiply_fusion.b_own, bf16[4,16,1280]{2,1,0:T(8,128)(2,1)} %pad.8.t_own, bf16[4,32,1280]{2,1,0:T(8,128)(2,1)} %bitcast.17), custom_call_target="tpu_custom_call" | custom-call | tf_op jit(solution)/shard_map/pallas_call | solution.py:396
  131.5 1.7 %copy.38 = f32[4,320,40]{1,2,0:T(8,128)} copy(f32[4,320,40]{1,2,0:T(8,128)} %bitcast.18) | data formatting | bytes 409600
  (6 shorter events, 0.1 us)
Async XLA Ops:
  0.0 6.9 %copy-start = (bf16[3,160,1280]{2,1,0:T(8,128)(2,1)S(1)}, bf16[3,160,1280]{2,1,0:T(8,128)(2,1)}, u32[]{:S(2)}) copy-start(bf16[3,160,1280]{2,1,0:T(8,128)(2,1)} %param.8) | copy-start | bytes 3686404
  1.8 3.5 %copy-start.2 = (s32[4,20,20]{2,0,1:T(4,128)S(1)}, s32[4,20,20]{2,0,1:T(4,128)}, u32[]{:S(2)}) copy-start(s32[4,20,20]{2,0,1:T(4,128)} %param.10) | copy-start | bytes 19204
  1.8 4.1 %copy-start.1 = (bf16[4,10,1280]{2,0,1:T(4,128)(2,1)S(1)}, bf16[4,10,1280]{2,0,1:T(4,128)(2,1)}, u32[]{:S(2)}) copy-start(bf16[4,10,1280]{2,0,1:T(4,128)(2,1)} %param.6) | copy-start | bytes 307204
  1.8 4.8 %copy-start.3 = (s32[4,2]{0,1:T(2,128)S(1)}, s32[4,2]{0,1:T(2,128)}, u32[]{:S(2)}) copy-start(s32[4,2]{0,1:T(2,128)} %param.9) | copy-start | bytes 100

commit v2 on v1

v2 whole, which is shorter than its diff:
```python
import jax
import jax.numpy as jnp
from jax import lax
from jax.experimental import pallas as pl
from jax.experimental.pallas import tpu as pltpu
from jax.sharding import PartitionSpec as P

MESH = pl.DeviceIdType.MESH
TILE = 64
V = 1280
VT = 20
BLK = 320
PIECE = 80
HALF = 640
EARLY = 768
WIDE = 384
PARTS = ((0, 0, WIDE), (1, WIDE, WIDE), (0, EARLY, 256), (1, EARLY + 256, 256))
NS = 2
SUB = BLK // NS
F32 = jnp.float32
BF16 = jnp.bfloat16


def kernel(
    b_in, t_in, occ_in, pairs, a_tiles, i_tiles, out,
    b_own, t_own, occ, l_own,
    bbuf, tst, tbuf, lbuf, ut, li2, xbuf, acc,
    s1, r1, s2, r2, fin, gbuf, hbuf,
    in_ls, t1_ss, t1_rs, tg_ss, tg_rs, th_ss, th_rs, l_ss, l_rs, own_ls,
    bo_ss, bf_ss, b_rs, sh_ss, sh_rs, p1_ss, p1_rs, p2_ss, p2_rs, g_ss, g_rs,
):
    x = lax.axis_index("col")
    row = lax.axis_index("row")
    k = lax.rem(row, 2)
    yz = row // 2
    y = yz // 4
    z = lax.rem(yz, 4)
    s = 1 - 2 * lax.rem(x, 2)
    xp = lax.rem(x + s + 4, 4)
    xm = lax.rem(x - s + 4, 4)
    xo = lax.rem(x + 2, 4)
    sg = 1 - 2 * k
    me8 = k * 4 + x
    pair = 2 * lax.rem(x, 2) + k
    sib = (yz * 2 + 1 - k, x)
    owner2 = lax.rem((x + 1) // 2 + 1, 2)
    is_owner = k == owner2
    main_j = x // 2

    def dev(yy, zz, kk, xx):
        return ((yy * 4 + zz) * 2 + kk, xx)

    def ring(v):
        return lax.rem(v + 8, 4)

    def peer8(d):
        idx = lax.rem(me8 + d, 8)
        return idx, idx // 4, lax.rem(idx, 4)

    def rcopy(src, dst, ss, rs, to):
        return pltpu.make_async_remote_copy(
            src_ref=src, dst_ref=dst, send_sem=ss, recv_sem=rs, device_id=to, device_id_type=MESH
        )

    pending = []

    def send(src, dst, ss, rs, to):
        c = rcopy(src, dst, ss, rs, to)
        c.start()
        pending.append(c)
        return c

    load_b = pltpu.make_async_copy(b_in, b_own, in_ls.at[0])
    load_b.start()
    load_occ = pltpu.make_async_copy(occ_in, occ, in_ls.at[1])
    load_occ.start()

    barrier = pltpu.get_barrier_semaphore()
    for d in range(1, 8):
        _, kk, xx = peer8(d)
        pl.semaphore_signal(barrier, inc=1, device_id=dev(y, z, kk, xx), device_id_type=MESH)
    for step in (1, -1):
        pl.semaphore_signal(barrier, inc=1, device_id=dev(ring(y + step), z, k, x), device_id_type=MESH)
        pl.semaphore_signal(barrier, inc=1, device_id=dev(y, ring(z + step), k, x), device_id_type=MESH)

    def iota(shape, dim):
        return lax.broadcasted_iota(jnp.int32, shape, dim)

    def ones(cond):
        return jnp.where(cond, 1.0, 0.0).astype(BF16)

    spread = ones(iota((VT, V), 0) == jnp.right_shift(iota((VT, V), 1), 6))
    first_row = (row * 4 + x) * 10
    pick_t = ones(jnp.right_shift(iota((16, VT), 0) + first_row, 6) == iota((16, VT), 1))
    for p in range(4):
        tiles = a_tiles[p].astype(F32).astype(BF16)
        small = jnp.dot(pick_t, tiles, preferred_element_type=F32).astype(BF16)
        mask = jnp.dot(small, spread, preferred_element_type=F32).astype(BF16)
        t_own[p] = jnp.zeros((16, V), BF16)
        t_own[p, 0:10] = t_in[p] * mask[0:10]
    pick_b = ones(iota((16, VT), 0) + 5 * x == iota((16, VT), 1))
    small = jnp.dot(pick_b, i_tiles[...].astype(F32).astype(BF16), preferred_element_type=F32).astype(BF16)
    mask = jnp.dot(small, spread, preferred_element_type=F32)
    load_b.wait()
    for t in range(BLK // TILE):
        wide = jnp.broadcast_to(mask[t:t + 1], (TILE, V)).astype(BF16)
        for j in range(3):
            b_own[j, t * TILE:(t + 1) * TILE] = b_own[j, t * TILE:(t + 1) * TILE] * wide
    pl.semaphore_wait(barrier, 11)

    for d in range(1, 8):
        idx, kk, xx = peer8(d)
        send(t_own.at[2 * lax.rem(xx, 2) + kk], tst.at[me8], t1_ss.at[d], t1_rs.at[d], dev(y, z, kk, xx))
    dest2 = jnp.where(is_owner, xm, xp)
    which2 = jnp.where(is_owner, 0, 2)

    def rows(i):
        return pl.ds(i * SUB, SUB)

    for i in range(NS):
        send(b_own.at[1 - main_j, rows(i)], bbuf.at[k, x, rows(i)], bo_ss.at[1, i], b_rs.at[0, 2, i],
             (row, xm))
    for i in range(NS):
        send(b_own.at[2, rows(i)], bbuf.at[2, x, rows(i)], bo_ss.at[2, i], b_rs.at[1, which2, i],
             (row, dest2))
    for i in range(NS):
        send(b_own.at[main_j, rows(i)], bbuf.at[k, x, rows(i)], bo_ss.at[0, i], b_rs.at[0, 0, i],
             (row, xp))

    def share(kind, pos, i, src=None):
        slot, blk = (k, None) if kind == 0 else (2, None)
        blk = (x, pos_main(pos) if kind == 0 else pos_second(pos))[pos > 0]
        dst = bbuf.at[slot, blk, rows(i)]
        return rcopy(dst if src is None else src, dst, sh_ss.at[kind, pos, i], sh_rs.at[kind, pos, i], sib)

    def pos_main(pos):
        return (x, xm, xp, xo)[pos]

    def pos_second(pos):
        return (x, xp, xm, xo)[pos]

    which_of = (None, 2, 0, 1)

    for i in range(NS):
        c = share(0, 0, i, b_own.at[main_j, rows(i)])
        c.start()
        pending.append(c)

    @pl.when(is_owner)
    def _():
        for i in range(NS):
            share(1, 0, i, b_own.at[2, rows(i)]).start()

    own_main = pltpu.make_async_copy(b_own.at[main_j], bbuf.at[k, x], own_ls.at[0])
    own_main.start()
    own_second = pltpu.make_async_copy(b_own.at[2], bbuf.at[2, x], own_ls.at[1])

    @pl.when(is_owner)
    def _():
        own_second.start()

    load_occ.wait()
    other = 2 * lax.rem(x, 2) + 1 - k
    orb_row, orb_col = iota((32, 480), 0), iota((32, 480), 1)

    def occ_rows(p):
        aux = jnp.bitwise_and(orb_row, 15)
        orb = jnp.where(orb_row < 16, pairs[p, 1], pairs[p, 0])
        hot = ones((orb_col == aux * 160 + orb) & (aux < 3))
        return jnp.dot(hot, occ[...].reshape(480, V), preferred_element_type=F32).astype(BF16)

    l_own[...] = occ_rows(other)
    lbuf[0] = occ_rows(pair)
    send(l_own, lbuf.at[1], l_ss, l_rs, sib)

    tst[me8] = t_own[pair]
    ri, ci = iota((PIECE, 128), 0), iota((PIECE, 128), 1)
    within = jnp.bitwise_and(ci, 15)
    pick = ones((within < 10) & (ri == jnp.right_shift(ci, 4) * 10 + within))
    for d in range(1, 8):
        src8 = lax.rem(me8 + 8 - d, 8)
        rcopy(t_own.at[0], tst.at[src8], t1_ss.at[d], t1_rs.at[d], sib).wait_recv()
    piece = jnp.dot(pick, tst[...].reshape(128, V), preferred_element_type=F32)
    tbuf[y, z] = piece.astype(BF16)

    col_h = (pl.ds(0, HALF), pl.ds(HALF, HALF))

    def along(half, phase, off):
        if (half == 0) == (phase == 0):
            return ring(y + off), dev(ring(y + off), z, k, x)
        return ring(z + off), dev(y, ring(z + off), k, x)

    def t_at(half, first, second):
        if half == 0:
            return tbuf.at[ring(y + first), ring(z + second), :, col_h[0]]
        return tbuf.at[ring(y + second), ring(z + first), :, col_h[1]]

    offs = (0, -sg, sg, 2)

    def t_one(half, n):
        ref = t_at(half, offs[n], 0)
        return ref, tg_ss.at[half, n], tg_rs.at[half, n]

    def t_two(half, m, n):
        ref = t_at(half, offs[m], offs[n])
        return ref, th_ss.at[half, m, n], th_rs.at[half, m, n]

    def t_spread(half, m):
        ref = t_at(half, offs[m], 0)
        send(ref, ref, th_ss.at[half, m, 0], th_rs.at[half, m, 1], along(half, 1, sg)[1])
        send(ref, ref, th_ss.at[half, m, 1], th_rs.at[half, m, 2], along(half, 1, -sg)[1])

    def t_arrive(ref, ss, rs):
        rcopy(ref, ref, ss, rs, sib).wait_recv()

    def t_first(m):
        for half in range(2):
            if m == 0:
                ref = t_at(half, 0, 0)
                send(ref, ref, tg_ss.at[half, 0], tg_rs.at[half, 1], along(half, 0, sg)[1])
                send(ref, ref, tg_ss.at[half, 1], tg_rs.at[half, 2], along(half, 0, -sg)[1])
            else:
                ref, ss, rs = t_one(half, m)
                t_arrive(ref, ss, rs)
                if m == 1:
                    send(ref, ref, tg_ss.at[half, 2], tg_rs.at[half, 3], along(half, 0, sg)[1])
            if m > 0:
                t_spread(half, m)
        if m == 0:
            for half in range(2):
                t_spread(half, 0)

    def t_second(m):
        for half in range(2):
            ref, ss, rs = t_two(half, m, 1)
            t_arrive(ref, ss, rs)
            send(ref, ref, th_ss.at[half, m, 2], th_rs.at[half, m, 3], along(half, 1, sg)[1])

    def t_finish(m):
        for half in range(2):
            for n in (2, 3):
                t_arrive(*t_two(half, m, n))

    for m in range(4):
        t_first(m)
    for m in range(4):
        t_second(m)

    def land(kind, pos):
        slot = k if kind == 0 else 2
        blk = pos_main(pos) if kind == 0 else pos_second(pos)
        for i in range(NS):
            ref = bbuf.at[slot, blk, rows(i)]
            rcopy(ref, ref, bo_ss.at[0, i], b_rs.at[kind, which_of[pos], i], sib).wait_recv()
            if pos == 1:
                to = xp if kind == 0 else xm
                rcopy(ref, ref, bf_ss.at[kind, i], b_rs.at[kind, 1, i], (row, to)).start()
            share(kind, pos, i).start()

    def from_sib(kind, pos):
        slot = 1 - k if kind == 0 else 2
        blk = pos_main(pos) if kind == 0 else pos_second(pos)
        for i in range(NS):
            ref = bbuf.at[slot, blk, rows(i)]
            rcopy(ref, ref, sh_ss.at[kind, pos, i], sh_rs.at[kind, pos, i], sib).wait_recv()

    def land_second(pos):
        @pl.when(is_owner)
        def _():
            land(1, pos)

    def from_owner(pos):
        @pl.when(jnp.logical_not(is_owner))
        def _():
            from_sib(1, pos)

    def blk_at(pos):
        off = jnp.where(pos == 1, -s, jnp.where(pos == 2, s, jnp.where(pos == 3, 2, 0)))
        return ring(x + off)

    def first_product(slot, pos):
        val = jnp.dot(bbuf[slot, blk_at(pos)], tbuf[...].reshape(V, V), preferred_element_type=F32)
        xbuf[slot, pl.ds(pl.multiple_of(pos * BLK, 64), BLK), :] = val.astype(BF16)

    def first_products(pos):
        @pl.loop(0, 3)
        def _(sl):
            first_product(sl, pos)

    nt = (((1,), (1,)), ((), ()))

    def second_product(pos, lo, width):
        blk = blk_at(pos)
        cols = pl.ds(lo, width)
        val = jnp.dot(ut[pl.ds(pl.multiple_of(blk * BLK, 64), BLK), :], li2[:, cols], preferred_element_type=F32)
        for sl in range(3):
            val += lax.dot_general(bbuf[sl, blk], xbuf[sl, cols, :], nt, preferred_element_type=F32)
        acc[blk, :, :, cols] = val.reshape(4, PIECE, width)

    land(0, 1)
    land_second(1)
    for m in range(4):
        t_finish(m)
    own_main.wait()

    @pl.when(is_owner)
    def _():
        own_second.wait()

    from_sib(0, 0)
    from_owner(0)
    first_products(0)

    rcopy(l_own, lbuf.at[1], l_ss, l_rs, sib).wait_recv()
    pick_l = jnp.where(k == x // 2, 0, 1)
    u = jnp.dot(lbuf[pick_l, 0:16], tbuf[...].reshape(V, V), preferred_element_type=F32)
    hi = u.astype(BF16).astype(F32)
    ut[...] = jnp.concatenate([hi, u - hi], axis=0).T.astype(BF16)
    li = lbuf[pick_l, 16:32]
    for n in range(4):
        blk = blk_at(n)
        for kk in range(4):
            @pl.when(blk == kk)
            def _():
                li2[0:16, n * BLK:(n + 1) * BLK] = li[:, kk * BLK:(kk + 1) * BLK]
                li2[16:32, n * BLK:(n + 1) * BLK] = li[:, kk * BLK:(kk + 1) * BLK]

    land(0, 2)
    land_second(2)
    from_sib(0, 1)
    from_owner(2)
    first_products(1)
    from_sib(0, 2)
    from_owner(1)
    first_products(2)

    @pl.loop(0, 3)
    def _(pos):
        second_product(pos, 0, EARLY)

    land(0, 3)
    land_second(3)
    first_product(k, 3)
    from_sib(0, 3)
    first_product(1 - k, 3)
    from_owner(3)
    first_product(2, 3)
    second_product(3, 0, EARLY)

    def late_product(lo, hi):
        @pl.loop(lo, hi)
        def _(pos):
            second_product(pos, EARLY, V - EARLY)

    def ralong(n, phase, off):
        return along(1 - PARTS[n][0], phase, off)

    def cols_of(n):
        return pl.ds(PARTS[n][1], PARTS[n][2])

    def part(n, t, i):
        if PARTS[n][0] == 0:
            return acc[t, i, :, cols_of(n)]
        return acc[i, t, :, cols_of(n)]

    def put(n, t, i, val):
        if PARTS[n][0] == 0:
            acc[t, i, :, cols_of(n)] = val
        else:
            acc[i, t, :, cols_of(n)] = val

    def p1_at(ref, n, m):
        return ref.at[n, m, :, :, pl.ds(0, PARTS[n][2])]

    def p2_at(ref, n, m):
        return ref.at[n, m, :, pl.ds(0, PARTS[n][2])]

    def p1_send(n, m, to):
        send(p1_at(s1, n, m), p1_at(r1, n, m), p1_ss.at[n, m], p1_rs.at[n, m], to)

    def p2_send(n, m, to):
        send(p2_at(s2, n, m), p2_at(r2, n, m), p2_ss.at[n, m], p2_rs.at[n, m], to)

    def p1_wait(n, m):
        rcopy(p1_at(s1, n, m), p1_at(r1, n, m), p1_ss.at[n, m], p1_rs.at[n, m], sib).wait_recv()

    def p2_wait(n, m):
        rcopy(p2_at(s2, n, m), p2_at(r2, n, m), p2_ss.at[n, m], p2_rs.at[n, m], sib).wait_recv()

    def got1(n, m, t):
        return r1[n, m, t, :, pl.ds(0, PARTS[n][2])].astype(F32)

    def got2(n, m):
        return r2[n, m, :, pl.ds(0, PARTS[n][2])].astype(F32)

    def p1_start(n):
        far = ralong(n, 0, 2)[0]
        back, back_dev = ralong(n, 0, -sg)
        for t in range(4):
            s1[n, 0, t, :, pl.ds(0, PARTS[n][2])] = part(n, t, far).astype(BF16)
        p1_send(n, 0, ralong(n, 0, sg)[1])
        for t in range(4):
            s1[n, 1, t, :, pl.ds(0, PARTS[n][2])] = part(n, t, back).astype(BF16)
        p1_send(n, 1, back_dev)

    def p1_middle(n):
        nxt, nxt_dev = ralong(n, 0, sg)
        p1_wait(n, 0)
        for t in range(4):
            s1[n, 2, t, :, pl.ds(0, PARTS[n][2])] = (part(n, t, nxt) + got1(n, 0, t)).astype(BF16)
        p1_send(n, 2, nxt_dev)

    def p1_end(n):
        here = ralong(n, 0, 0)[0]
        p1_wait(n, 1)
        p1_wait(n, 2)

        def total(t):
            return part(n, t, here) + got1(n, 1, t) + got1(n, 2, t)

        far = ralong(n, 1, 2)[0]
        back, back_dev = ralong(n, 1, -sg)
        nxt, nxt_dev = ralong(n, 1, sg)
        s2[n, 0, :, pl.ds(0, PARTS[n][2])] = total(far).astype(BF16)
        p2_send(n, 0, nxt_dev)
        s2[n, 1, :, pl.ds(0, PARTS[n][2])] = total(back).astype(BF16)
        p2_send(n, 1, back_dev)
        put(n, nxt, here, total(nxt))
        mid = ralong(n, 1, 0)[0]
        put(n, mid, here, total(mid))

    def p2_middle(n):
        nxt, nxt_dev = ralong(n, 1, sg)
        here = ralong(n, 0, 0)[0]
        p2_wait(n, 0)
        s2[n, 2, :, pl.ds(0, PARTS[n][2])] = (part(n, nxt, here) + got2(n, 0)).astype(BF16)
        p2_send(n, 2, nxt_dev)

    def p2_end(n):
        mid = ralong(n, 1, 0)[0]
        here = ralong(n, 0, 0)[0]
        p2_wait(n, 1)
        p2_wait(n, 2)
        fin[:, cols_of(n)] = part(n, mid, here) + got2(n, 1) + got2(n, 2)
        xx = blk_at(n)
        for kk in range(2):
            gbuf[n, kk] = fin[kk * 40:(kk + 1) * 40, n * BLK:(n + 1) * BLK]
        if n == 0:
            send(gbuf.at[0, 1 - k], hbuf.at[me8], g_ss.at[0, 0], g_rs.at[me8], sib)
            hbuf[me8] = gbuf[0, k]
        else:
            for kk in range(2):
                send(gbuf.at[n, kk], hbuf.at[me8], g_ss.at[n, kk], g_rs.at[me8], dev(y, z, kk, xx))

    p1_start(0)
    p1_start(1)
    late_product(0, 2)
    p1_middle(0)
    p1_middle(1)
    late_product(2, 4)
    p1_start(2)
    p1_start(3)
    p1_end(0)
    p1_end(1)
    p2_middle(0)
    p2_middle(1)
    p1_middle(2)
    p1_middle(3)
    p2_end(0)
    p2_end(1)
    p1_end(2)
    p1_end(3)
    p2_middle(2)
    p2_middle(3)
    p2_end(2)
    p2_end(3)

    for d in range(1, 8):
        src8 = lax.rem(me8 + d, 8)
        rcopy(gbuf.at[0, 0], hbuf.at[src8], g_ss.at[0, 0], g_rs.at[src8], sib).wait_recv()
    for p in range(4):
        src = (p % 2) * 4 + p // 2
        out[p] = hbuf[src] + hbuf[src + 2]

    for c in pending:
        c.wait_send()

    def wait_own(kind, pos_list):
        for pos in pos_list:
            for i in range(NS):
                share(kind, pos, i).wait_send()
        for i in range(NS):
            ref = bbuf.at[k if kind == 0 else 2, xm if kind == 0 else xp, rows(i)]
            rcopy(ref, ref, bf_ss.at[kind, i], b_rs.at[kind, 1, i], (row, xp if kind == 0 else xm)).wait_send()

    wait_own(0, (1, 2, 3))

    @pl.when(is_owner)
    def _():
        wait_own(1, (0, 1, 2, 3))


def exchange(*args):
    vmem = pl.BlockSpec(memory_space=pltpu.VMEM)
    anywhere = pl.BlockSpec(memory_space=pl.ANY)
    smem = pl.BlockSpec(memory_space=pltpu.SMEM)
    dma = pltpu.SemaphoreType.DMA
    return pl.pallas_call(
        kernel,
        out_shape=jax.ShapeDtypeStruct((4, 40, BLK), F32),
        in_specs=[anywhere, vmem, anywhere, smem, vmem, vmem],
        out_specs=vmem,
        scratch_shapes=[
            pltpu.VMEM((3, BLK, V), BF16),
            pltpu.VMEM((4, 16, V), BF16),
            pltpu.VMEM((3, 160, V), BF16),
            pltpu.VMEM((32, V), BF16),
            pltpu.VMEM((3, 4, BLK, V), BF16),
            pltpu.VMEM((8, 16, V), BF16),
            pltpu.VMEM((4, 4, PIECE, V), BF16),
            pltpu.VMEM((2, 32, V), BF16),
            pltpu.VMEM((V, 32), BF16),
            pltpu.VMEM((32, V), BF16),
            pltpu.VMEM((3, V, V), BF16),
            pltpu.VMEM((4, 4, PIECE, V), F32),
            pltpu.VMEM((4, 3, 4, PIECE, WIDE), BF16),
            pltpu.VMEM((4, 3, 4, PIECE, WIDE), BF16),
            pltpu.VMEM((4, 3, PIECE, WIDE), BF16),
            pltpu.VMEM((4, 3, PIECE, WIDE), BF16),
            pltpu.VMEM((PIECE, V), F32),
            pltpu.VMEM((4, 2, 40, BLK), F32),
            pltpu.VMEM((8, 40, BLK), F32),
            dma((2,)),
            dma((8,)), dma((8,)),
            dma((2, 4)), dma((2, 4)),
            dma((2, 4, 4)), dma((2, 4, 4)),
            dma, dma,
            dma((2,)),
            dma((3, NS)), dma((2, NS)), dma((2, 3, NS)),
            dma((2, 4, NS)), dma((2, 4, NS)),
            dma((4, 3)), dma((4, 3)), dma((4, 3)), dma((4, 3)),
            dma((4, 2)), dma((8,)),
        ],
        compiler_params=pltpu.CompilerParams(
            collective_id=0, has_side_effects=True, vmem_limit_bytes=62 * 1024 * 1024
        ),
    )(*args)


def local(
    amplitudes, integrals, occupied_integrals, pair_orbitals, amplitude_tiles, integral_tiles
):
    res = exchange(
        integrals, amplitudes, occupied_integrals, pair_orbitals, amplitude_tiles, integral_tiles
    )
    return jnp.swapaxes(res, 1, 2)


def solution(mesh):
    placed = (
        P(None, ("row", "col"), None),
        P("row", "col", None),
        P("row", None, None),
        P(),
        P(),
        P(),
    )
    return jax.shard_map(
        local, mesh=mesh, in_specs=placed, out_specs=P(None, "col", "row"), check_vma=False
    )
```

time: 134 us -> 118 us (0.88)
  Pallas kernels: 123 us -> 112 us
  other arithmetic: 4.31 us -> 0 us
    pallas_call x1, Pallas kernels: 123 us -> 112 us  [exchange(): pl.pallas_call(kernel, out_shape=jax.ShapeDtypeStruct((4, 40, BLK), F32),...]
    unnamed x10 -> x4, local copies, waits for them, and re-layouts: 1.72 us -> 5.97 us
    mul x2 -> x0, other arithmetic: 3.49 us -> none  [the longest x1 3.43 us: local(): masked_int = integrals * factor_mask.astype(BF16)[None]]
    pad x2 -> x0, local copies, waits for them, and re-layouts: 1.43 us -> none  [the longest x1 0.75 us: local(): occ = jnp.pad(occ, ((0, 0), (0, 13), (0, 0))).reshape(4, 32, V)]
where the time goes in v2:
time: 118 us
  Pallas kernels  112 us (95%)
  local copies, waits for them, and re-layouts  5.97 us (5%)
    pallas_call x1, Pallas kernels, exchange(): pl.pallas_call(kernel, out_shape=jax.ShapeDtypeStruct((4, 40, BLK), F32),...  112 us
    unnamed x4, local copies, waits for them, and re-layouts  5.97 us

profile of v2, /device:TPU:1, one launch (start us, length us, event | category | flops | bytes accessed | tf_op | source)
XLA Modules:
  0.0 118.2 jit_solution(4753887877848389085)
XLA Ops:
  0.0 1.4 %copy.8.pairs = s32[4,2]{1,0:T(4,128)} copy(s32[4,2]{0,1:T(2,128)} %param.9) | data formatting | bytes 64 | tf_op args[3]
  1.4 1.4 %copy.9.a_tiles = s32[4,20,20]{2,1,0:T(8,128)} copy(s32[4,20,20]{2,0,1:T(4,128)} %param.10) | data formatting | bytes 12800 | tf_op args[4]
  2.7 1.6 %copy.7.t_in = bf16[4,10,1280]{2,1,0:T(8,128)(2,1)} copy(bf16[4,10,1280]{2,0,1:T(4,128)(2,1)} %param.6) | data formatting | bytes 204800 | tf_op args[0]
  4.3 112.2 %shard_map.64 = f32[4,40,320]{2,1,0:T(8,128)} custom-call(bf16[3,320,1280]{2,1,0:T(8,128)(2,1)} %b_in.1, bf16[4,10,1280]{2,1,0:T(8,128)(2,1)} %copy.7.t_in, bf16[3,160,1280]{2,1,0:T(8,128)(2,1)} %occ_in.1, s32[4,2]{1,0:T(4,128)} %copy.8.pairs, s32[4,20,20]{2,1,0:T(8,128)} %copy.9.a_tiles, s32[20,20]{1,0:T(8,128)} %i_tiles.1), custom_call_target="tpu_custom_call" | custom-call | tf_op jit(solution)/shard_map/pallas_call | solution.py:508
  116.5 1.7 %copy.11 = f32[4,320,40]{1,2,0:T(8,128)} copy(f32[4,320,40]{1,2,0:T(8,128)} %bitcast.1) | data formatting | bytes 409600

commit v3 on v2

--- a/solution.py
+++ b/solution.py
@@ -12,9 +12,9 @@
 BLK = 320
 PIECE = 80
 HALF = 640
-EARLY = 768
-WIDE = 384
-PARTS = ((0, 0, WIDE), (1, WIDE, WIDE), (0, EARLY, 256), (1, EARLY + 256, 256))
+EARLY = 896
+WIDE = 512
+PARTS = ((0, 0, 384), (1, 384, WIDE), (0, EARLY, 256), (1, EARLY + 256, 128))
 NS = 2
 SUB = BLK // NS
 F32 = jnp.float32
@@ -90,14 +90,17 @@
         return jnp.where(cond, 1.0, 0.0).astype(BF16)
 
     spread = ones(iota((VT, V), 0) == jnp.right_shift(iota((VT, V), 1), 6))
-    first_row = (row * 4 + x) * 10
-    pick_t = ones(jnp.right_shift(iota((16, VT), 0) + first_row, 6) == iota((16, VT), 1))
+    tile_row = jnp.right_shift(jnp.right_shift(iota((40, 80), 0), 2) + (row * 4 + x) * 10, 6)
+    same_pair = jnp.bitwise_and(iota((40, 80), 0), 3) == jnp.bitwise_and(iota((40, 80), 1), 3)
+    pick_t = ones(same_pair & (jnp.right_shift(iota((40, 80), 1), 2) == tile_row))
+    small = jnp.dot(pick_t, a_tiles[...].astype(F32).astype(BF16), preferred_element_type=F32).astype(BF16)
+    mask = jnp.dot(small, spread, preferred_element_type=F32)
+    raw = jnp.concatenate([t_in[i].astype(F32) for i in range(10)], axis=0)
+    turn_i = jnp.bitwise_and(iota((64, 40), 0), 15)
+    turn = ones((turn_i < 10) & (iota((64, 40), 1) == turn_i * 4 + jnp.right_shift(iota((64, 40), 0), 4)))
+    turned = jnp.dot(turn, (raw * mask).astype(BF16), preferred_element_type=F32).astype(BF16)
     for p in range(4):
-        tiles = a_tiles[p].astype(F32).astype(BF16)
-        small = jnp.dot(pick_t, tiles, preferred_element_type=F32).astype(BF16)
-        mask = jnp.dot(small, spread, preferred_element_type=F32).astype(BF16)
-        t_own[p] = jnp.zeros((16, V), BF16)
-        t_own[p, 0:10] = t_in[p] * mask[0:10]
+        t_own[p] = turned[p * 16:(p + 1) * 16]
     pick_b = ones(iota((16, VT), 0) + 5 * x == iota((16, VT), 1))
     small = jnp.dot(pick_b, i_tiles[...].astype(F32).astype(BF16), preferred_element_type=F32).astype(BF16)
     mask = jnp.dot(small, spread, preferred_element_type=F32)
@@ -117,6 +120,59 @@
     def rows(i):
         return pl.ds(i * SUB, SUB)
 
+    def share(kind, pos, i, src=None):
+        slot, blk = (k, None) if kind == 0 else (2, None)
+        blk = (x, pos_main(pos) if kind == 0 else pos_second(pos))[pos > 0]
+        dst = bbuf.at[slot, blk, rows(i)]
+        return rcopy(dst if src is None else src, dst, sh_ss.at[kind, pos, i], sh_rs.at[kind, pos, i], sib)
+
+    def pos_main(pos):
+        return (x, xm, xp, xo)[pos]
+
+    def pos_second(pos):
+        return (x, xp, xm, xo)[pos]
+
+    which_of = (None, 2, 0, 1)
+
+    for i in range(NS):
+        c = share(0, 0, i, b_own.at[main_j, rows(i)])
+        c.start()
+        pending.append(c)
+
+    @pl.when(is_owner)
+    def _():
+        for i in range(NS):
+            share(1, 0, i, b_own.at[2, rows(i)]).start()
+
+    own_main = pltpu.make_async_copy(b_own.at[main_j], bbuf.at[k, x], own_ls.at[0])
+    own_main.start()
+    own_second = pltpu.make_async_copy(b_own.at[2], bbuf.at[2, x], own_ls.at[1])
+
+    @pl.when(is_owner)
+    def _():
+        own_second.start()
+
+    load_occ.wait()
+    other = 2 * lax.rem(x, 2) + 1 - k
+    orb_row, orb_col = iota((32, 480), 0), iota((32, 480), 1)
+
+    def occ_rows(p):
+        aux = jnp.bitwise_and(orb_row, 15)
+        orb = jnp.where(orb_row < 16, pairs[1, p], pairs[0, p])
+        hot = ones((orb_col == aux * 160 + orb) & (aux < 3))
+        return jnp.dot(hot, occ[...].reshape(480, V), preferred_element_type=F32).astype(BF16)
+
+    l_own[...] = occ_rows(other)
+    lbuf[0] = occ_rows(pair)
+    send(l_own, lbuf.at[1], l_ss, l_rs, sib)
+
+    tst[me8] = t_own[pair]
+    ri, ci = iota((PIECE, 128), 0), iota((PIECE, 128), 1)
+    within = jnp.bitwise_and(ci, 15)
+    pick = ones((within < 10) & (ri == jnp.right_shift(ci, 4) * 10 + within))
+    for d in range(1, 8):
+        src8 = lax.rem(me8 + 8 - d, 8)
+        rcopy(t_own.at[0], tst.at[src8], t1_ss.at[d], t1_rs.at[d], sib).wait_recv()
     for i in range(NS):
         send(b_own.at[1 - main_j, rows(i)], bbuf.at[k, x, rows(i)], bo_ss.at[1, i], b_rs.at[0, 2, i],
              (row, xm))
@@ -127,59 +183,6 @@
         send(b_own.at[main_j, rows(i)], bbuf.at[k, x, rows(i)], bo_ss.at[0, i], b_rs.at[0, 0, i],
              (row, xp))
 
-    def share(kind, pos, i, src=None):
-        slot, blk = (k, None) if kind == 0 else (2, None)
-        blk = (x, pos_main(pos) if kind == 0 else pos_second(pos))[pos > 0]
-        dst = bbuf.at[slot, blk, rows(i)]
-        return rcopy(dst if src is None else src, dst, sh_ss.at[kind, pos, i], sh_rs.at[kind, pos, i], sib)
-
-    def pos_main(pos):
-        return (x, xm, xp, xo)[pos]
-
-    def pos_second(pos):
-        return (x, xp, xm, xo)[pos]
-
-    which_of = (None, 2, 0, 1)
-
-    for i in range(NS):
-        c = share(0, 0, i, b_own.at[main_j, rows(i)])
-        c.start()
-        pending.append(c)
-
-    @pl.when(is_owner)
-    def _():
-        for i in range(NS):
-            share(1, 0, i, b_own.at[2, rows(i)]).start()
-
-    own_main = pltpu.make_async_copy(b_own.at[main_j], bbuf.at[k, x], own_ls.at[0])
-    own_main.start()
-    own_second = pltpu.make_async_copy(b_own.at[2], bbuf.at[2, x], own_ls.at[1])
-
-    @pl.when(is_owner)
-    def _():
-        own_second.start()
-
-    load_occ.wait()
-    other = 2 * lax.rem(x, 2) + 1 - k
-    orb_row, orb_col = iota((32, 480), 0), iota((32, 480), 1)
-
-    def occ_rows(p):
-        aux = jnp.bitwise_and(orb_row, 15)
-        orb = jnp.where(orb_row < 16, pairs[p, 1], pairs[p, 0])
-        hot = ones((orb_col == aux * 160 + orb) & (aux < 3))
-        return jnp.dot(hot, occ[...].reshape(480, V), preferred_element_type=F32).astype(BF16)
-
-    l_own[...] = occ_rows(other)
-    lbuf[0] = occ_rows(pair)
-    send(l_own, lbuf.at[1], l_ss, l_rs, sib)
-
-    tst[me8] = t_own[pair]
-    ri, ci = iota((PIECE, 128), 0), iota((PIECE, 128), 1)
-    within = jnp.bitwise_and(ci, 15)
-    pick = ones((within < 10) & (ri == jnp.right_shift(ci, 4) * 10 + within))
-    for d in range(1, 8):
-        src8 = lax.rem(me8 + 8 - d, 8)
-        rcopy(t_own.at[0], tst.at[src8], t1_ss.at[d], t1_rs.at[d], sib).wait_recv()
     piece = jnp.dot(pick, tst[...].reshape(128, V), preferred_element_type=F32)
     tbuf[y, z] = piece.astype(BF16)
 
@@ -274,6 +277,19 @@
         def _():
             from_sib(1, pos)
 
+    slot_b, slot_a = owner2, 1 - owner2
+
+    def get_main(owner_gathers, pos):
+        gathers = is_owner if owner_gathers else jnp.logical_not(is_owner)
+
+        @pl.when(gathers)
+        def _():
+            land(0, pos)
+
+        @pl.when(jnp.logical_not(gathers))
+        def _():
+            from_sib(0, pos)
+
     def blk_at(pos):
         off = jnp.where(pos == 1, -s, jnp.where(pos == 2, s, jnp.where(pos == 3, 2, 0)))
         return ring(x + off)
@@ -297,61 +313,6 @@
             val += lax.dot_general(bbuf[sl, blk], xbuf[sl, cols, :], nt, preferred_element_type=F32)
         acc[blk, :, :, cols] = val.reshape(4, PIECE, width)
 
-    land(0, 1)
-    land_second(1)
-    for m in range(4):
-        t_finish(m)
-    own_main.wait()
-
-    @pl.when(is_owner)
-    def _():
-        own_second.wait()
-
-    from_sib(0, 0)
-    from_owner(0)
-    first_products(0)
-
-    rcopy(l_own, lbuf.at[1], l_ss, l_rs, sib).wait_recv()
-    pick_l = jnp.where(k == x // 2, 0, 1)
-    u = jnp.dot(lbuf[pick_l, 0:16], tbuf[...].reshape(V, V), preferred_element_type=F32)
-    hi = u.astype(BF16).astype(F32)
-    ut[...] = jnp.concatenate([hi, u - hi], axis=0).T.astype(BF16)
-    li = lbuf[pick_l, 16:32]
-    for n in range(4):
-        blk = blk_at(n)
-        for kk in range(4):
-            @pl.when(blk == kk)
-            def _():
-                li2[0:16, n * BLK:(n + 1) * BLK] = li[:, kk * BLK:(kk + 1) * BLK]
-                li2[16:32, n * BLK:(n + 1) * BLK] = li[:, kk * BLK:(kk + 1) * BLK]
-
-    land(0, 2)
-    land_second(2)
-    from_sib(0, 1)
-    from_owner(2)
-    first_products(1)
-    from_sib(0, 2)
-    from_owner(1)
-    first_products(2)
-
-    @pl.loop(0, 3)
-    def _(pos):
-        second_product(pos, 0, EARLY)
-
-    land(0, 3)
-    land_second(3)
-    first_product(k, 3)
-    from_sib(0, 3)
-    first_product(1 - k, 3)
-    from_owner(3)
-    first_product(2, 3)
-    second_product(3, 0, EARLY)
-
-    def late_product(lo, hi):
-        @pl.loop(lo, hi)
-        def _(pos):
-            second_product(pos, EARLY, V - EARLY)
-
     def ralong(n, phase, off):
         return along(1 - PARTS[n][0], phase, off)
 
@@ -375,15 +336,9 @@
     def p2_at(ref, n, m):
         return ref.at[n, m, :, pl.ds(0, PARTS[n][2])]
 
-    def p1_send(n, m, to):
-        send(p1_at(s1, n, m), p1_at(r1, n, m), p1_ss.at[n, m], p1_rs.at[n, m], to)
-
     def p2_send(n, m, to):
         send(p2_at(s2, n, m), p2_at(r2, n, m), p2_ss.at[n, m], p2_rs.at[n, m], to)
 
-    def p1_wait(n, m):
-        rcopy(p1_at(s1, n, m), p1_at(r1, n, m), p1_ss.at[n, m], p1_rs.at[n, m], sib).wait_recv()
-
     def p2_wait(n, m):
         rcopy(p2_at(s2, n, m), p2_at(r2, n, m), p2_ss.at[n, m], p2_rs.at[n, m], sib).wait_recv()
 
@@ -393,22 +348,82 @@
     def got2(n, m):
         return r2[n, m, :, pl.ds(0, PARTS[n][2])].astype(F32)
 
-    def p1_start(n):
-        far = ralong(n, 0, 2)[0]
-        back, back_dev = ralong(n, 0, -sg)
-        for t in range(4):
-            s1[n, 0, t, :, pl.ds(0, PARTS[n][2])] = part(n, t, far).astype(BF16)
-        p1_send(n, 0, ralong(n, 0, sg)[1])
-        for t in range(4):
-            s1[n, 1, t, :, pl.ds(0, PARTS[n][2])] = part(n, t, back).astype(BF16)
-        p1_send(n, 1, back_dev)
+    def width(n):
+        return pl.ds(0, PARTS[n][2])
+
+    def row_at(ref, n, m, t):
+        return ref.at[n, m, t, :, width(n)]
+
+    def row_copy(n, m, pos, to):
+        t = blk_at(pos)
+        return rcopy(row_at(s1, n, m, t), row_at(r1, n, m, t), p1_ss.at[n, m, pos], p1_rs.at[n, m, pos], to)
+
+    def send_rows(n, pos):
+        t = blk_at(pos)
+        s1[n, 0, t, :, width(n)] = part(n, t, ralong(n, 0, 2)[0]).astype(BF16)
+        row_copy(n, 0, pos, ralong(n, 0, sg)[1]).start()
+        s1[n, 1, t, :, width(n)] = part(n, t, ralong(n, 0, -sg)[0]).astype(BF16)
+        row_copy(n, 1, pos, ralong(n, 0, -sg)[1]).start()
+
+    def middle_rows(n, lo, hi):
+        nxt, nxt_dev = ralong(n, 0, sg)
+
+        @pl.loop(lo, hi)
+        def _(pos):
+            t = blk_at(pos)
+            row_copy(n, 0, pos, sib).wait_recv()
+            s1[n, 2, t, :, width(n)] = (part(n, t, nxt) + r1[n, 0, t, :, width(n)].astype(F32)).astype(BF16)
+            row_copy(n, 2, pos, nxt_dev).start()
+
+    def blk_copy(n, m, to):
+        return rcopy(p1_at(s1, n, m), p1_at(r1, n, m), p1_ss.at[n, m, 0], p1_rs.at[n, m, 0], to)
+
+    def send_block(n, pos):
+        blk = blk_at(pos)
+        for m, off, to in ((0, 2, sg), (1, -sg, -sg)):
+            @pl.when(blk == ralong(n, 0, off)[0])
+            def _():
+                for t in range(4):
+                    s1[n, m, t, :, width(n)] = acc[blk, t, :, cols_of(n)].astype(BF16)
+                blk_copy(n, m, ralong(n, 0, to)[1]).start()
 
     def p1_middle(n):
         nxt, nxt_dev = ralong(n, 0, sg)
-        p1_wait(n, 0)
+        blk_copy(n, 0, sib).wait_recv()
         for t in range(4):
-            s1[n, 2, t, :, pl.ds(0, PARTS[n][2])] = (part(n, t, nxt) + got1(n, 0, t)).astype(BF16)
-        p1_send(n, 2, nxt_dev)
+            s1[n, 2, t, :, width(n)] = (part(n, t, nxt) + got1(n, 0, t)).astype(BF16)
+        blk_copy(n, 2, nxt_dev).start()
+
+    def p1_wait(n, m):
+        if PARTS[n][0] == 0:
+            @pl.loop(0, 4)
+            def _(pos):
+                row_copy(n, m, pos, sib).wait_recv()
+        else:
+            blk_copy(n, m, sib).wait_recv()
+
+    def early_product(lo, hi):
+        @pl.loop(lo, hi)
+        def _(pos):
+            second_product(pos, 0, EARLY)
+            send_rows(0, pos)
+            send_block(1, pos)
+
+    def late_product(lo, hi):
+        @pl.loop(lo, hi)
+        def _(pos):
+            second_product(pos, EARLY, V - EARLY)
+            send_rows(2, pos)
+            send_block(3, pos)
+
+    def p1_sent(n):
+        for m in range(3):
+            if PARTS[n][0] == 0:
+                @pl.loop(0, 4)
+                def _(pos):
+                    row_copy(n, m, pos, sib).wait_send()
+            else:
+                blk_copy(n, m, sib).wait_send()
 
     def p1_end(n):
         here = ralong(n, 0, 0)[0]
@@ -452,19 +467,72 @@
             for kk in range(2):
                 send(gbuf.at[n, kk], hbuf.at[me8], g_ss.at[n, kk], g_rs.at[me8], dev(y, z, kk, xx))
 
-    p1_start(0)
-    p1_start(1)
+    land(0, 1)
+    land_second(1)
+    for m in range(4):
+        t_finish(m)
+    own_main.wait()
+
+    @pl.when(is_owner)
+    def _():
+        own_second.wait()
+
+    from_sib(0, 0)
+    from_owner(0)
+    first_products(0)
+
+    rcopy(l_own, lbuf.at[1], l_ss, l_rs, sib).wait_recv()
+    pick_l = jnp.where(k == x // 2, 0, 1)
+    u = jnp.dot(lbuf[pick_l, 0:16], tbuf[...].reshape(V, V), preferred_element_type=F32)
+    hi = u.astype(BF16).astype(F32)
+    ut[...] = jnp.concatenate([hi, u - hi], axis=0).T.astype(BF16)
+    li = lbuf[pick_l, 16:32]
+    for n in range(4):
+        blk = blk_at(n)
+        for kk in range(4):
+            @pl.when(blk == kk)
+            def _():
+                li2[0:16, n * BLK:(n + 1) * BLK] = li[:, kk * BLK:(kk + 1) * BLK]
+                li2[16:32, n * BLK:(n + 1) * BLK] = li[:, kk * BLK:(kk + 1) * BLK]
+
+    from_sib(0, 1)
+
+    @pl.loop(0, 2)
+    def _(i):
+        first_product(jnp.where(i == 0, slot_b, slot_a), 1)
+
+    get_main(True, 2)
+    first_product(slot_b, 2)
+    from_owner(1)
+    first_product(2, 2)
+    land_second(2)
+    from_owner(2)
+    first_product(2, 1)
+    get_main(False, 2)
+    first_product(slot_a, 2)
+    early_product(0, 1)
+    land_second(3)
+    get_main(True, 3)
+    from_owner(3)
+
+    @pl.loop(0, 2)
+    def _(i):
+        first_product(jnp.where(i == 0, 2, slot_b), 3)
+
+    early_product(1, 3)
+    get_main(False, 3)
+    first_product(slot_a, 3)
+    middle_rows(0, 0, 3)
+    early_product(3, 4)
     late_product(0, 2)
-    p1_middle(0)
+    middle_rows(0, 3, 4)
     p1_middle(1)
     late_product(2, 4)
-    p1_start(2)
-    p1_start(3)
     p1_end(0)
     p1_end(1)
     p2_middle(0)
     p2_middle(1)
-    p1_middle(2)
+    middle_rows(2, 0, 4)
     p1_middle(3)
     p2_end(0)
     p2_end(1)
@@ -484,6 +552,8 @@
 
     for c in pending:
         c.wait_send()
+    for n in range(4):
+        p1_sent(n)
 
     def wait_own(kind, pos_list):
         for pos in pos_list:
@@ -538,7 +608,7 @@
             dma((2,)),
             dma((3, NS)), dma((2, NS)), dma((2, 3, NS)),
             dma((2, 4, NS)), dma((2, 4, NS)),
-            dma((4, 3)), dma((4, 3)), dma((4, 3)), dma((4, 3)),
+            dma((4, 3, 4)), dma((4, 3, 4)), dma((4, 3)), dma((4, 3)),
             dma((4, 2)), dma((8,)),
         ],
         compiler_params=pltpu.CompilerParams(
@@ -551,7 +621,12 @@
     amplitudes, integrals, occupied_integrals, pair_orbitals, amplitude_tiles, integral_tiles
 ):
     res = exchange(
-        integrals, amplitudes, occupied_integrals, pair_orbitals, amplitude_tiles, integral_tiles
+        integrals,
+        jnp.swapaxes(amplitudes, 0, 1),
+        occupied_integrals,
+        pair_orbitals.T,
+        jnp.swapaxes(amplitude_tiles, 0, 1).reshape(80, 20),
+        integral_tiles,
     )
     return jnp.swapaxes(res, 1, 2)
 

time: 118 us -> 121 us (1.025); the launches traced: 118 us -> 120 us
  Pallas kernels: 112 us -> 118 us
  local copies, waits for them, and re-layouts: 5.97 us -> 1.65 us
    pallas_call x1, Pallas kernels: 112 us -> 118 us  [exchange(): pl.pallas_call(kernel, out_shape=jax.ShapeDtypeStruct((4, 40, BLK), F32),...]
    unnamed x4 -> x1, local copies, waits for them, and re-layouts: 5.97 us -> 1.65 us
where the time goes in v3:
time: 121 us; the launch traced here: 120 us
  Pallas kernels  118 us (98%)
  local copies, waits for them, and re-layouts  1.65 us (1%)
    pallas_call x1, Pallas kernels, exchange(): pl.pallas_call(kernel, out_shape=jax.ShapeDtypeStruct((4, 40, BLK), F32),...  118 us

profile of v3, /device:TPU:1, one launch (start us, length us, event | category | flops | bytes accessed | tf_op | source)
XLA Modules:
  0.0 119.8 jit_solution(17627638634321368423)
XLA Ops:
  0.0 118.1 %shard_map.64 = f32[4,40,320]{2,1,0:T(8,128)} custom-call(bf16[3,320,1280]{2,1,0:T(8,128)(2,1)} %b_in.1, bf16[10,4,1280]{2,1,0:T(4,128)(2,1)} %bitcast.7, bf16[3,160,1280]{2,1,0:T(8,128)(2,1)} %occ_in.1, s32[2,4]{1,0:T(2,128)} %bitcast.9, s32[80,20]{1,0:T(8,128)} %bitcast.8, s32[20,20]{1,0:T(8,128)} %i_tiles.1), custom_call_target="tpu_custom_call" | custom-call | tf_op jit(solution)/shard_map/pallas_call | solution.py:578
  118.1 1.7 %copy.8 = f32[4,320,40]{1,2,0:T(8,128)} copy(f32[4,320,40]{1,2,0:T(8,128)} %bitcast.6) | data formatting | bytes 409600

commit v4 on v3

--- a/solution.py
+++ b/solution.py
@@ -12,9 +12,16 @@
 BLK = 320
 PIECE = 80
 HALF = 640
-EARLY = 896
-WIDE = 512
-PARTS = ((0, 0, 384), (1, 384, WIDE), (0, EARLY, 256), (1, EARLY + 256, 128))
+EARLY = 768
+WIDE = 384
+PARTS = ((0, 0, WIDE), (1, WIDE, WIDE), (1, EARLY, WIDE), (0, EARLY + WIDE, 128))
+OWN, XM, XP, XO = range(4)
+LAID = (
+    ((0, 0, 320),),
+    ((640, 0, 128), (1088, 128, 192)),
+    ((320, 0, 320),),
+    ((768, 0, 320),),
+)
 NS = 2
 SUB = BLK // NS
 F32 = jnp.float32
@@ -120,59 +127,6 @@
     def rows(i):
         return pl.ds(i * SUB, SUB)
 
-    def share(kind, pos, i, src=None):
-        slot, blk = (k, None) if kind == 0 else (2, None)
-        blk = (x, pos_main(pos) if kind == 0 else pos_second(pos))[pos > 0]
-        dst = bbuf.at[slot, blk, rows(i)]
-        return rcopy(dst if src is None else src, dst, sh_ss.at[kind, pos, i], sh_rs.at[kind, pos, i], sib)
-
-    def pos_main(pos):
-        return (x, xm, xp, xo)[pos]
-
-    def pos_second(pos):
-        return (x, xp, xm, xo)[pos]
-
-    which_of = (None, 2, 0, 1)
-
-    for i in range(NS):
-        c = share(0, 0, i, b_own.at[main_j, rows(i)])
-        c.start()
-        pending.append(c)
-
-    @pl.when(is_owner)
-    def _():
-        for i in range(NS):
-            share(1, 0, i, b_own.at[2, rows(i)]).start()
-
-    own_main = pltpu.make_async_copy(b_own.at[main_j], bbuf.at[k, x], own_ls.at[0])
-    own_main.start()
-    own_second = pltpu.make_async_copy(b_own.at[2], bbuf.at[2, x], own_ls.at[1])
-
-    @pl.when(is_owner)
-    def _():
-        own_second.start()
-
-    load_occ.wait()
-    other = 2 * lax.rem(x, 2) + 1 - k
-    orb_row, orb_col = iota((32, 480), 0), iota((32, 480), 1)
-
-    def occ_rows(p):
-        aux = jnp.bitwise_and(orb_row, 15)
-        orb = jnp.where(orb_row < 16, pairs[1, p], pairs[0, p])
-        hot = ones((orb_col == aux * 160 + orb) & (aux < 3))
-        return jnp.dot(hot, occ[...].reshape(480, V), preferred_element_type=F32).astype(BF16)
-
-    l_own[...] = occ_rows(other)
-    lbuf[0] = occ_rows(pair)
-    send(l_own, lbuf.at[1], l_ss, l_rs, sib)
-
-    tst[me8] = t_own[pair]
-    ri, ci = iota((PIECE, 128), 0), iota((PIECE, 128), 1)
-    within = jnp.bitwise_and(ci, 15)
-    pick = ones((within < 10) & (ri == jnp.right_shift(ci, 4) * 10 + within))
-    for d in range(1, 8):
-        src8 = lax.rem(me8 + 8 - d, 8)
-        rcopy(t_own.at[0], tst.at[src8], t1_ss.at[d], t1_rs.at[d], sib).wait_recv()
     for i in range(NS):
         send(b_own.at[1 - main_j, rows(i)], bbuf.at[k, x, rows(i)], bo_ss.at[1, i], b_rs.at[0, 2, i],
              (row, xm))
@@ -183,6 +137,59 @@
         send(b_own.at[main_j, rows(i)], bbuf.at[k, x, rows(i)], bo_ss.at[0, i], b_rs.at[0, 0, i],
              (row, xp))
 
+    def share(kind, pos, i, src=None):
+        slot, blk = (k, None) if kind == 0 else (2, None)
+        blk = (x, pos_main(pos) if kind == 0 else pos_second(pos))[pos > 0]
+        dst = bbuf.at[slot, blk, rows(i)]
+        return rcopy(dst if src is None else src, dst, sh_ss.at[kind, pos, i], sh_rs.at[kind, pos, i], sib)
+
+    def pos_main(pos):
+        return (x, xm, xp, xo)[pos]
+
+    def pos_second(pos):
+        return (x, xp, xm, xo)[pos]
+
+    which_of = (None, 2, 0, 1)
+
+    for i in range(NS):
+        c = share(0, 0, i, b_own.at[main_j, rows(i)])
+        c.start()
+        pending.append(c)
+
+    @pl.when(is_owner)
+    def _():
+        for i in range(NS):
+            share(1, 0, i, b_own.at[2, rows(i)]).start()
+
+    own_main = pltpu.make_async_copy(b_own.at[main_j], bbuf.at[k, x], own_ls.at[0])
+    own_main.start()
+    own_second = pltpu.make_async_copy(b_own.at[2], bbuf.at[2, x], own_ls.at[1])
+
+    @pl.when(is_owner)
+    def _():
+        own_second.start()
+
+    load_occ.wait()
+    other = 2 * lax.rem(x, 2) + 1 - k
+    orb_row, orb_col = iota((32, 480), 0), iota((32, 480), 1)
+
+    def occ_rows(p):
+        aux = jnp.bitwise_and(orb_row, 15)
+        orb = jnp.where(orb_row < 16, pairs[1, p], pairs[0, p])
+        hot = ones((orb_col == aux * 160 + orb) & (aux < 3))
+        return jnp.dot(hot, occ[...].reshape(480, V), preferred_element_type=F32).astype(BF16)
+
+    l_own[...] = occ_rows(other)
+    lbuf[0] = occ_rows(pair)
+    send(l_own, lbuf.at[1], l_ss, l_rs, sib)
+
+    tst[me8] = t_own[pair]
+    ri, ci = iota((PIECE, 128), 0), iota((PIECE, 128), 1)
+    within = jnp.bitwise_and(ci, 15)
+    pick = ones((within < 10) & (ri == jnp.right_shift(ci, 4) * 10 + within))
+    for d in range(1, 8):
+        src8 = lax.rem(me8 + 8 - d, 8)
+        rcopy(t_own.at[0], tst.at[src8], t1_ss.at[d], t1_rs.at[d], sib).wait_recv()
     piece = jnp.dot(pick, tst[...].reshape(128, V), preferred_element_type=F32)
     tbuf[y, z] = piece.astype(BF16)
 
@@ -296,7 +303,8 @@
 
     def first_product(slot, pos):
         val = jnp.dot(bbuf[slot, blk_at(pos)], tbuf[...].reshape(V, V), preferred_element_type=F32)
-        xbuf[slot, pl.ds(pl.multiple_of(pos * BLK, 64), BLK), :] = val.astype(BF16)
+        for col, r, m in LAID[pos]:
+            xbuf[slot, col:col + m, :] = val[r:r + m].astype(BF16)
 
     def first_products(pos):
         @pl.loop(0, 3)
@@ -305,8 +313,7 @@
 
     nt = (((1,), (1,)), ((), ()))
 
-    def second_product(pos, lo, width):
-        blk = blk_at(pos)
+    def second_product(blk, lo, width):
         cols = pl.ds(lo, width)
         val = jnp.dot(ut[pl.ds(pl.multiple_of(blk * BLK, 64), BLK), :], li2[:, cols], preferred_element_type=F32)
         for sl in range(3):
@@ -354,32 +361,29 @@
     def row_at(ref, n, m, t):
         return ref.at[n, m, t, :, width(n)]
 
-    def row_copy(n, m, pos, to):
-        t = blk_at(pos)
-        return rcopy(row_at(s1, n, m, t), row_at(r1, n, m, t), p1_ss.at[n, m, pos], p1_rs.at[n, m, pos], to)
-
-    def send_rows(n, pos):
-        t = blk_at(pos)
+    def row_copy(n, m, t, to):
+        return rcopy(row_at(s1, n, m, t), row_at(r1, n, m, t), p1_ss.at[n, m, t], p1_rs.at[n, m, t], to)
+
+    def send_rows(n, t):
         s1[n, 0, t, :, width(n)] = part(n, t, ralong(n, 0, 2)[0]).astype(BF16)
-        row_copy(n, 0, pos, ralong(n, 0, sg)[1]).start()
+        row_copy(n, 0, t, ralong(n, 0, sg)[1]).start()
         s1[n, 1, t, :, width(n)] = part(n, t, ralong(n, 0, -sg)[0]).astype(BF16)
-        row_copy(n, 1, pos, ralong(n, 0, -sg)[1]).start()
-
-    def middle_rows(n, lo, hi):
+        row_copy(n, 1, t, ralong(n, 0, -sg)[1]).start()
+
+    def middle_rows(n, lo, hi, order):
         nxt, nxt_dev = ralong(n, 0, sg)
 
         @pl.loop(lo, hi)
         def _(pos):
-            t = blk_at(pos)
-            row_copy(n, 0, pos, sib).wait_recv()
+            t = order(pos)
+            row_copy(n, 0, t, sib).wait_recv()
             s1[n, 2, t, :, width(n)] = (part(n, t, nxt) + r1[n, 0, t, :, width(n)].astype(F32)).astype(BF16)
-            row_copy(n, 2, pos, nxt_dev).start()
+            row_copy(n, 2, t, nxt_dev).start()
 
     def blk_copy(n, m, to):
         return rcopy(p1_at(s1, n, m), p1_at(r1, n, m), p1_ss.at[n, m, 0], p1_rs.at[n, m, 0], to)
 
-    def send_block(n, pos):
-        blk = blk_at(pos)
+    def send_block(n, blk):
         for m, off, to in ((0, 2, sg), (1, -sg, -sg)):
             @pl.when(blk == ralong(n, 0, off)[0])
             def _():
@@ -405,16 +409,21 @@
     def early_product(lo, hi):
         @pl.loop(lo, hi)
         def _(pos):
-            second_product(pos, 0, EARLY)
-            send_rows(0, pos)
-            send_block(1, pos)
+            blk = blk_at(pos)
+            second_product(blk, 0, EARLY)
+            send_rows(0, blk)
+            send_block(1, blk)
+
+    def y_order(pos):
+        return ring(y + jnp.where(pos == 0, 2, jnp.where(pos == 1, -sg, jnp.where(pos == 2, sg, 0))))
 
     def late_product(lo, hi):
         @pl.loop(lo, hi)
         def _(pos):
-            second_product(pos, EARLY, V - EARLY)
-            send_rows(2, pos)
-            send_block(3, pos)
+            blk = y_order(pos)
+            second_product(blk, EARLY, V - EARLY)
+            send_rows(3, blk)
+            send_block(2, blk)
 
     def p1_sent(n):
         for m in range(3):
@@ -457,9 +466,11 @@
         p2_wait(n, 1)
         p2_wait(n, 2)
         fin[:, cols_of(n)] = part(n, mid, here) + got2(n, 1) + got2(n, 2)
-        xx = blk_at(n)
+        place = (OWN, XP, XO, XM)[n]
+        xx = blk_at(place)
         for kk in range(2):
-            gbuf[n, kk] = fin[kk * 40:(kk + 1) * 40, n * BLK:(n + 1) * BLK]
+            for col, r, m in LAID[place]:
+                gbuf[n, kk, :, r:r + m] = fin[kk * 40:(kk + 1) * 40, col:col + m]
         if n == 0:
             send(gbuf.at[0, 1 - k], hbuf.at[me8], g_ss.at[0, 0], g_rs.at[me8], sib)
             hbuf[me8] = gbuf[0, k]
@@ -492,8 +503,9 @@
         for kk in range(4):
             @pl.when(blk == kk)
             def _():
-                li2[0:16, n * BLK:(n + 1) * BLK] = li[:, kk * BLK:(kk + 1) * BLK]
-                li2[16:32, n * BLK:(n + 1) * BLK] = li[:, kk * BLK:(kk + 1) * BLK]
+                for col, r, m in LAID[n]:
+                    li2[0:16, col:col + m] = li[:, kk * BLK + r:kk * BLK + r + m]
+                    li2[16:32, col:col + m] = li[:, kk * BLK + r:kk * BLK + r + m]
 
     from_sib(0, 1)
 
@@ -501,44 +513,56 @@
     def _(i):
         first_product(jnp.where(i == 0, slot_b, slot_a), 1)
 
-    get_main(True, 2)
-    first_product(slot_b, 2)
+    get_main(False, 2)
+    first_product(slot_a, 2)
     from_owner(1)
     first_product(2, 2)
     land_second(2)
     from_owner(2)
     first_product(2, 1)
-    get_main(False, 2)
-    first_product(slot_a, 2)
-    early_product(0, 1)
+    get_main(True, 2)
+    first_product(slot_b, 2)
     land_second(3)
-    get_main(True, 3)
+    get_main(False, 3)
     from_owner(3)
 
     @pl.loop(0, 2)
     def _(i):
-        first_product(jnp.where(i == 0, 2, slot_b), 3)
-
-    early_product(1, 3)
-    get_main(False, 3)
-    first_product(slot_a, 3)
-    middle_rows(0, 0, 3)
+        first_product(jnp.where(i == 0, 2, slot_a), 3)
+
+    early_product(0, 2)
+
+    @pl.when(is_owner)
+    def _():
+        land(0, 3)
+
+    early_product(2, 3)
+
+    @pl.when(jnp.logical_not(is_owner))
+    def _():
+        from_sib(0, 3)
+
+    first_product(slot_b, 3)
     early_product(3, 4)
-    late_product(0, 2)
-    middle_rows(0, 3, 4)
+    middle_rows(0, 0, 3, blk_at)
+    late_product(0, 1)
     p1_middle(1)
-    late_product(2, 4)
+    middle_rows(0, 3, 4, blk_at)
+    late_product(1, 3)
+    p1_middle(2)
+    middle_rows(3, 0, 1, y_order)
+    late_product(3, 4)
     p1_end(0)
+    middle_rows(3, 1, 3, y_order)
     p1_end(1)
+    middle_rows(3, 3, 4, y_order)
     p2_middle(0)
+    p1_end(2)
     p2_middle(1)
-    middle_rows(2, 0, 4)
-    p1_middle(3)
+    p1_end(3)
     p2_end(0)
+    p2_middle(2)
     p2_end(1)
-    p1_end(2)
-    p1_end(3)
-    p2_middle(2)
     p2_middle(3)
     p2_end(2)
     p2_end(3)

time: 121 us -> 104 us (0.86)
  Pallas kernels: 118 us -> 102 us
    pallas_call x1, Pallas kernels: 118 us -> 102 us  [exchange(): pl.pallas_call(kernel, out_shape=jax.ShapeDtypeStruct((4, 40, BLK), F32),...]
where the time goes in v4:
time: 104 us; the launch traced here: 103 us
  Pallas kernels  102 us (98%)
  local copies, waits for them, and re-layouts  1.65 us (2%)
    pallas_call x1, Pallas kernels, exchange(): pl.pallas_call(kernel, out_shape=jax.ShapeDtypeStruct((4, 40, BLK), F32),...  102 us

profile of v4, /device:TPU:1, one launch (start us, length us, event | category | flops | bytes accessed | tf_op | source)
XLA Modules:
  0.0 103.4 jit_solution(7727333058205278717)
XLA Ops:
  0.0 101.8 %shard_map.64 = f32[4,40,320]{2,1,0:T(8,128)} custom-call(bf16[3,320,1280]{2,1,0:T(8,128)(2,1)} %b_in.1, bf16[10,4,1280]{2,1,0:T(4,128)(2,1)} %bitcast.7, bf16[3,160,1280]{2,1,0:T(8,128)(2,1)} %occ_in.1, s32[2,4]{1,0:T(2,128)} %bitcast.9, s32[80,20]{1,0:T(8,128)} %bitcast.8, s32[20,20]{1,0:T(8,128)} %i_tiles.1), custom_call_target="tpu_custom_call" | custom-call | tf_op jit(solution)/shard_map/pallas_call | solution.py:602
  101.8 1.7 %copy.8 = f32[4,320,40]{1,2,0:T(8,128)} copy(f32[4,320,40]{1,2,0:T(8,128)} %bitcast.6) | data formatting | bytes 409600

commit v5 on v4

--- a/solution.py
+++ b/solution.py
@@ -14,11 +14,11 @@
 HALF = 640
 EARLY = 768
 WIDE = 384
-PARTS = ((0, 0, WIDE), (1, WIDE, WIDE), (1, EARLY, WIDE), (0, EARLY + WIDE, 128))
+PARTS = ((0, 0, WIDE), (1, WIDE, WIDE), (1, EARLY, 256), (0, EARLY + 256, 256))
 OWN, XM, XP, XO = range(4)
 LAID = (
+    ((640, 0, 128), (1088, 128, 192)),
     ((0, 0, 320),),
-    ((640, 0, 128), (1088, 128, 192)),
     ((320, 0, 320),),
     ((768, 0, 320),),
 )
@@ -86,7 +86,7 @@
     for d in range(1, 8):
         _, kk, xx = peer8(d)
         pl.semaphore_signal(barrier, inc=1, device_id=dev(y, z, kk, xx), device_id_type=MESH)
-    for step in (1, -1):
+    for step in (1, 2, -1):
         pl.semaphore_signal(barrier, inc=1, device_id=dev(ring(y + step), z, k, x), device_id_type=MESH)
         pl.semaphore_signal(barrier, inc=1, device_id=dev(y, ring(z + step), k, x), device_id_type=MESH)
 
@@ -116,7 +116,7 @@
         wide = jnp.broadcast_to(mask[t:t + 1], (TILE, V)).astype(BF16)
         for j in range(3):
             b_own[j, t * TILE:(t + 1) * TILE] = b_own[j, t * TILE:(t + 1) * TILE] * wide
-    pl.semaphore_wait(barrier, 11)
+    pl.semaphore_wait(barrier, 13)
 
     for d in range(1, 8):
         idx, kk, xx = peer8(d)
@@ -301,15 +301,15 @@
         off = jnp.where(pos == 1, -s, jnp.where(pos == 2, s, jnp.where(pos == 3, 2, 0)))
         return ring(x + off)
 
+    def pick_pos(pos, values):
+        return jnp.where(pos == 0, values[0], jnp.where(pos == 1, values[1], jnp.where(pos == 2, values[2], values[3])))
+
     def first_product(slot, pos):
         val = jnp.dot(bbuf[slot, blk_at(pos)], tbuf[...].reshape(V, V), preferred_element_type=F32)
-        for col, r, m in LAID[pos]:
-            xbuf[slot, col:col + m, :] = val[r:r + m].astype(BF16)
-
-    def first_products(pos):
-        @pl.loop(0, 3)
-        def _(sl):
-            first_product(sl, pos)
+        one = pl.multiple_of(pick_pos(pos, (640, 0, 320, 768)), 64)
+        two = pl.multiple_of(pick_pos(pos, (1088, 128, 448, 896)), 64)
+        xbuf[slot, pl.ds(one, 128), :] = val[0:128].astype(BF16)
+        xbuf[slot, pl.ds(two, 192), :] = val[128:320].astype(BF16)
 
     nt = (((1,), (1,)), ((), ()))
 
@@ -331,241 +331,206 @@
             return acc[t, i, :, cols_of(n)]
         return acc[i, t, :, cols_of(n)]
 
-    def put(n, t, i, val):
-        if PARTS[n][0] == 0:
-            acc[t, i, :, cols_of(n)] = val
-        else:
-            acc[i, t, :, cols_of(n)] = val
-
     def p1_at(ref, n, m):
         return ref.at[n, m, :, :, pl.ds(0, PARTS[n][2])]
 
     def p2_at(ref, n, m):
         return ref.at[n, m, :, pl.ds(0, PARTS[n][2])]
 
-    def p2_send(n, m, to):
-        send(p2_at(s2, n, m), p2_at(r2, n, m), p2_ss.at[n, m], p2_rs.at[n, m], to)
-
-    def p2_wait(n, m):
-        rcopy(p2_at(s2, n, m), p2_at(r2, n, m), p2_ss.at[n, m], p2_rs.at[n, m], sib).wait_recv()
-
     def got1(n, m, t):
         return r1[n, m, t, :, pl.ds(0, PARTS[n][2])].astype(F32)
 
     def got2(n, m):
         return r2[n, m, :, pl.ds(0, PARTS[n][2])].astype(F32)
 
+    hops = (2, -1, 1)
+
     def width(n):
         return pl.ds(0, PARTS[n][2])
 
-    def row_at(ref, n, m, t):
-        return ref.at[n, m, t, :, width(n)]
-
-    def row_copy(n, m, t, to):
-        return rcopy(row_at(s1, n, m, t), row_at(r1, n, m, t), p1_ss.at[n, m, t], p1_rs.at[n, m, t], to)
+    def row_copy(n, m, t):
+        at = (n, m, t, slice(None), width(n))
+        return rcopy(s1.at[at], r1.at[at], p1_ss.at[n, m, t], p1_rs.at[n, m, t], ralong(n, 0, hops[m])[1])
 
     def send_rows(n, t):
-        s1[n, 0, t, :, width(n)] = part(n, t, ralong(n, 0, 2)[0]).astype(BF16)
-        row_copy(n, 0, t, ralong(n, 0, sg)[1]).start()
-        s1[n, 1, t, :, width(n)] = part(n, t, ralong(n, 0, -sg)[0]).astype(BF16)
-        row_copy(n, 1, t, ralong(n, 0, -sg)[1]).start()
-
-    def middle_rows(n, lo, hi, order):
-        nxt, nxt_dev = ralong(n, 0, sg)
-
-        @pl.loop(lo, hi)
-        def _(pos):
-            t = order(pos)
-            row_copy(n, 0, t, sib).wait_recv()
-            s1[n, 2, t, :, width(n)] = (part(n, t, nxt) + r1[n, 0, t, :, width(n)].astype(F32)).astype(BF16)
-            row_copy(n, 2, t, nxt_dev).start()
-
-    def blk_copy(n, m, to):
-        return rcopy(p1_at(s1, n, m), p1_at(r1, n, m), p1_ss.at[n, m, 0], p1_rs.at[n, m, 0], to)
+        for m in range(3):
+            s1[n, m, t, :, width(n)] = part(n, t, ralong(n, 0, hops[m])[0]).astype(BF16)
+            row_copy(n, m, t).start()
+
+    def blk_copy(n, m):
+        return rcopy(p1_at(s1, n, m), p1_at(r1, n, m), p1_ss.at[n, m, 0], p1_rs.at[n, m, 0],
+                     ralong(n, 0, hops[m])[1])
 
     def send_block(n, blk):
-        for m, off, to in ((0, 2, sg), (1, -sg, -sg)):
-            @pl.when(blk == ralong(n, 0, off)[0])
+        for m in range(3):
+            @pl.when(blk == ralong(n, 0, hops[m])[0])
             def _():
                 for t in range(4):
                     s1[n, m, t, :, width(n)] = acc[blk, t, :, cols_of(n)].astype(BF16)
-                blk_copy(n, m, ralong(n, 0, to)[1]).start()
-
-    def p1_middle(n):
-        nxt, nxt_dev = ralong(n, 0, sg)
-        blk_copy(n, 0, sib).wait_recv()
-        for t in range(4):
-            s1[n, 2, t, :, width(n)] = (part(n, t, nxt) + got1(n, 0, t)).astype(BF16)
-        blk_copy(n, 2, nxt_dev).start()
-
-    def p1_wait(n, m):
-        if PARTS[n][0] == 0:
-            @pl.loop(0, 4)
-            def _(pos):
-                row_copy(n, m, pos, sib).wait_recv()
+                blk_copy(n, m).start()
+
+    def p1_each(n, what):
+        for m in range(3):
+            if PARTS[n][0] == 0:
+                @pl.loop(0, 4)
+                def _(t):
+                    what(row_copy(n, m, t))
+            else:
+                what(blk_copy(n, m))
+
+    def y_order(pos):
+        return ring(y + jnp.where(pos == 0, 2, jnp.where(pos == 1, -1, jnp.where(pos == 2, 1, 0))))
+
+    def p1_end(n):
+        here = ralong(n, 0, 0)[0]
+        p1_each(n, lambda c: c.wait_recv())
+
+        def total(t):
+            return (part(n, t, here) + got1(n, 0, t)) + (got1(n, 1, t) + got1(n, 2, t))
+
+        for m in range(3):
+            there, there_dev = ralong(n, 1, hops[m])
+            s2[n, m, :, width(n)] = total(there).astype(BF16)
+            send(p2_at(s2, n, m), p2_at(r2, n, m), p2_ss.at[n, m], p2_rs.at[n, m], there_dev)
+        fin[:, cols_of(n)] = total(ralong(n, 1, 0)[0])
+
+    def p2_end(n):
+        for m in range(3):
+            rcopy(p2_at(s2, n, m), p2_at(r2, n, m), p2_ss.at[n, m], p2_rs.at[n, m], sib).wait_recv()
+        fin[:, cols_of(n)] = (fin[:, cols_of(n)] + got2(n, 0)) + (got2(n, 1) + got2(n, 2))
+
+    def x_send(place):
+        xx = blk_at(place)
+        for kk in range(2):
+            for col, r, m in LAID[place]:
+                gbuf[place, kk, :, r:r + m] = fin[kk * 40:(kk + 1) * 40, col:col + m]
+        if place == OWN:
+            send(gbuf.at[OWN, 1 - k], hbuf.at[me8], g_ss.at[OWN, 0], g_rs.at[me8], sib)
+            hbuf[me8] = gbuf[OWN, k]
         else:
-            blk_copy(n, m, sib).wait_recv()
-
-    def early_product(lo, hi):
-        @pl.loop(lo, hi)
-        def _(pos):
-            blk = blk_at(pos)
+            for kk in range(2):
+                send(gbuf.at[place, kk], hbuf.at[me8], g_ss.at[place, kk], g_rs.at[me8], dev(y, z, kk, xx))
+
+    def cycle_terms():
+        rcopy(l_own, lbuf.at[1], l_ss, l_rs, sib).wait_recv()
+        pick_l = jnp.where(k == x // 2, 0, 1)
+        u = jnp.dot(lbuf[pick_l, 0:16], tbuf[...].reshape(V, V), preferred_element_type=F32)
+        hi = u.astype(BF16).astype(F32)
+        ut[...] = jnp.concatenate([hi, u - hi], axis=0).T.astype(BF16)
+        li = lbuf[pick_l, 16:32]
+        for n in range(4):
+            blk = blk_at(n)
+            for kk in range(4):
+                @pl.when(blk == kk)
+                def _():
+                    for col, r, m in LAID[n]:
+                        li2[0:16, col:col + m] = li[:, kk * BLK + r:kk * BLK + r + m]
+                        li2[16:32, col:col + m] = li[:, kk * BLK + r:kk * BLK + r + m]
+
+    def gatherer(owner):
+        return pl.when(is_owner if owner else jnp.logical_not(is_owner))
+
+    land(0, 1)
+    land_second(1)
+
+    @gatherer(False)
+    def _():
+        land(0, 2)
+
+    for m in range(4):
+        t_finish(m)
+    own_main.wait()
+
+    @gatherer(True)
+    def _():
+        own_second.wait()
+
+    from_sib(0, 0)
+    from_owner(0)
+
+    @pl.loop(0, 16)
+    def _(step):
+        @pl.when(step == 3)
+        def _():
+            cycle_terms()
+            from_sib(0, 1)
+            land_second(2)
+
+        @pl.when(step == 5)
+        def _():
+            @gatherer(True)
+            def _():
+                from_sib(0, 2)
+
+        @pl.when(step == 6)
+        def _():
+            from_owner(1)
+
+        @pl.when(step == 7)
+        def _():
+            from_owner(2)
+
+        @pl.when(step == 8)
+        def _():
+            get_main(True, 2)
+
+        @pl.when(step == 9)
+        def _():
+            land_second(3)
+            from_owner(3)
+
+        @pl.when(step == 10)
+        def _():
+            get_main(False, 3)
+
+        @pl.when(step == 13)
+        def _():
+            @gatherer(True)
+            def _():
+                land(0, 3)
+
+        @pl.when(step == 14)
+        def _():
+            @gatherer(False)
+            def _():
+                from_sib(0, 3)
+
+        late_slot = jnp.where((step == 4) | (step == 5) | (step == 10), slot_a, 2)
+        slot = jnp.where(step < 3, step, jnp.where((step == 3) | (step == 8) | (step == 14), slot_b, late_slot))
+        late_pos = jnp.where((step == 5) | (step == 6) | (step == 8), 2, 3)
+        pos = jnp.where(step < 3, 0, jnp.where((step == 3) | (step == 4) | (step == 7), 1, late_pos))
+        summing = ((step >= 11) & (step < 14)) | (step == 15)
+
+        @pl.when(jnp.logical_not(summing))
+        def _():
+            first_product(slot, pos)
+
+        @pl.when(summing)
+        def _():
+            blk = blk_at(jnp.where(step == 15, 3, step - 11))
             second_product(blk, 0, EARLY)
             send_rows(0, blk)
             send_block(1, blk)
 
-    def y_order(pos):
-        return ring(y + jnp.where(pos == 0, 2, jnp.where(pos == 1, -sg, jnp.where(pos == 2, sg, 0))))
-
-    def late_product(lo, hi):
-        @pl.loop(lo, hi)
-        def _(pos):
-            blk = y_order(pos)
-            second_product(blk, EARLY, V - EARLY)
-            send_rows(3, blk)
-            send_block(2, blk)
-
-    def p1_sent(n):
-        for m in range(3):
-            if PARTS[n][0] == 0:
-                @pl.loop(0, 4)
-                def _(pos):
-                    row_copy(n, m, pos, sib).wait_send()
-            else:
-                blk_copy(n, m, sib).wait_send()
-
-    def p1_end(n):
-        here = ralong(n, 0, 0)[0]
-        p1_wait(n, 1)
-        p1_wait(n, 2)
-
-        def total(t):
-            return part(n, t, here) + got1(n, 1, t) + got1(n, 2, t)
-
-        far = ralong(n, 1, 2)[0]
-        back, back_dev = ralong(n, 1, -sg)
-        nxt, nxt_dev = ralong(n, 1, sg)
-        s2[n, 0, :, pl.ds(0, PARTS[n][2])] = total(far).astype(BF16)
-        p2_send(n, 0, nxt_dev)
-        s2[n, 1, :, pl.ds(0, PARTS[n][2])] = total(back).astype(BF16)
-        p2_send(n, 1, back_dev)
-        put(n, nxt, here, total(nxt))
-        mid = ralong(n, 1, 0)[0]
-        put(n, mid, here, total(mid))
-
-    def p2_middle(n):
-        nxt, nxt_dev = ralong(n, 1, sg)
-        here = ralong(n, 0, 0)[0]
-        p2_wait(n, 0)
-        s2[n, 2, :, pl.ds(0, PARTS[n][2])] = (part(n, nxt, here) + got2(n, 0)).astype(BF16)
-        p2_send(n, 2, nxt_dev)
-
-    def p2_end(n):
-        mid = ralong(n, 1, 0)[0]
-        here = ralong(n, 0, 0)[0]
-        p2_wait(n, 1)
-        p2_wait(n, 2)
-        fin[:, cols_of(n)] = part(n, mid, here) + got2(n, 1) + got2(n, 2)
-        place = (OWN, XP, XO, XM)[n]
-        xx = blk_at(place)
-        for kk in range(2):
-            for col, r, m in LAID[place]:
-                gbuf[n, kk, :, r:r + m] = fin[kk * 40:(kk + 1) * 40, col:col + m]
-        if n == 0:
-            send(gbuf.at[0, 1 - k], hbuf.at[me8], g_ss.at[0, 0], g_rs.at[me8], sib)
-            hbuf[me8] = gbuf[0, k]
-        else:
-            for kk in range(2):
-                send(gbuf.at[n, kk], hbuf.at[me8], g_ss.at[n, kk], g_rs.at[me8], dev(y, z, kk, xx))
-
-    land(0, 1)
-    land_second(1)
-    for m in range(4):
-        t_finish(m)
-    own_main.wait()
-
-    @pl.when(is_owner)
-    def _():
-        own_second.wait()
-
-    from_sib(0, 0)
-    from_owner(0)
-    first_products(0)
-
-    rcopy(l_own, lbuf.at[1], l_ss, l_rs, sib).wait_recv()
-    pick_l = jnp.where(k == x // 2, 0, 1)
-    u = jnp.dot(lbuf[pick_l, 0:16], tbuf[...].reshape(V, V), preferred_element_type=F32)
-    hi = u.astype(BF16).astype(F32)
-    ut[...] = jnp.concatenate([hi, u - hi], axis=0).T.astype(BF16)
-    li = lbuf[pick_l, 16:32]
-    for n in range(4):
-        blk = blk_at(n)
-        for kk in range(4):
-            @pl.when(blk == kk)
-            def _():
-                for col, r, m in LAID[n]:
-                    li2[0:16, col:col + m] = li[:, kk * BLK + r:kk * BLK + r + m]
-                    li2[16:32, col:col + m] = li[:, kk * BLK + r:kk * BLK + r + m]
-
-    from_sib(0, 1)
-
-    @pl.loop(0, 2)
-    def _(i):
-        first_product(jnp.where(i == 0, slot_b, slot_a), 1)
-
-    get_main(False, 2)
-    first_product(slot_a, 2)
-    from_owner(1)
-    first_product(2, 2)
-    land_second(2)
-    from_owner(2)
-    first_product(2, 1)
-    get_main(True, 2)
-    first_product(slot_b, 2)
-    land_second(3)
-    get_main(False, 3)
-    from_owner(3)
-
-    @pl.loop(0, 2)
-    def _(i):
-        first_product(jnp.where(i == 0, 2, slot_a), 3)
-
-    early_product(0, 2)
-
-    @pl.when(is_owner)
-    def _():
-        land(0, 3)
-
-    early_product(2, 3)
-
-    @pl.when(jnp.logical_not(is_owner))
-    def _():
-        from_sib(0, 3)
-
-    first_product(slot_b, 3)
-    early_product(3, 4)
-    middle_rows(0, 0, 3, blk_at)
-    late_product(0, 1)
-    p1_middle(1)
-    middle_rows(0, 3, 4, blk_at)
-    late_product(1, 3)
-    p1_middle(2)
-    middle_rows(3, 0, 1, y_order)
-    late_product(3, 4)
+    @pl.loop(0, 4)
+    def _(pos):
+        blk = y_order(pos)
+        second_product(blk, EARLY, V - EARLY)
+        send_rows(3, blk)
+        send_block(2, blk)
+
     p1_end(0)
-    middle_rows(3, 1, 3, y_order)
     p1_end(1)
-    middle_rows(3, 3, 4, y_order)
-    p2_middle(0)
     p1_end(2)
-    p2_middle(1)
     p1_end(3)
     p2_end(0)
-    p2_middle(2)
+    x_send(XM)
     p2_end(1)
-    p2_middle(3)
+    x_send(XP)
     p2_end(2)
     p2_end(3)
+    x_send(XO)
+    x_send(OWN)
 
     for d in range(1, 8):
         src8 = lax.rem(me8 + d, 8)
@@ -577,7 +542,7 @@
     for c in pending:
         c.wait_send()
     for n in range(4):
-        p1_sent(n)
+        p1_each(n, lambda c: c.wait_send())
 
     def wait_own(kind, pos_list):
         for pos in pos_list:

time: 104 us -> 105 us (level)
  no operation moved by 1% of the time
where the time goes in v5:
time: 105 us; the launch traced here: 104 us
  Pallas kernels  103 us (98%)
  local copies, waits for them, and re-layouts  1.65 us (2%)
    pallas_call x1, Pallas kernels, exchange(): pl.pallas_call(kernel, out_shape=jax.ShapeDtypeStruct((4, 40, BLK), F32),...  103 us

profile of v5, /device:TPU:1, one launch (start us, length us, event | category | flops | bytes accessed | tf_op | source)
XLA Modules:
  0.0 104.5 jit_solution(4379336726567459480)
XLA Ops:
  0.0 102.8 %shard_map.64 = f32[4,40,320]{2,1,0:T(8,128)} custom-call(bf16[3,320,1280]{2,1,0:T(8,128)(2,1)} %b_in.1, bf16[10,4,1280]{2,1,0:T(4,128)(2,1)} %bitcast.7, bf16[3,160,1280]{2,1,0:T(8,128)(2,1)} %occ_in.1, s32[2,4]{1,0:T(2,128)} %bitcast.9, s32[80,20]{1,0:T(8,128)} %bitcast.8, s32[20,20]{1,0:T(8,128)} %i_tiles.1), custom_call_target="tpu_custom_call" | custom-call | tf_op jit(solution)/shard_map/pallas_call | solution.py:567
  102.8 1.7 %copy.8 = f32[4,320,40]{1,2,0:T(8,128)} copy(f32[4,320,40]{1,2,0:T(8,128)} %bitcast.6) | data formatting | bytes 409600

commit v6 on v5

--- a/solution.py
+++ b/solution.py
@@ -13,8 +13,8 @@
 PIECE = 80
 HALF = 640
 EARLY = 768
-WIDE = 384
-PARTS = ((0, 0, WIDE), (1, WIDE, WIDE), (1, EARLY, 256), (0, EARLY + 256, 256))
+WIDE = 512
+PARTS = ((0, 0, WIDE), (0, WIDE, 256), (1, EARLY, 384), (0, EARLY + 384, 128))
 OWN, XM, XP, XO = range(4)
 LAID = (
     ((640, 0, 128), (1088, 128, 192)),
@@ -286,17 +286,6 @@
 
     slot_b, slot_a = owner2, 1 - owner2
 
-    def get_main(owner_gathers, pos):
-        gathers = is_owner if owner_gathers else jnp.logical_not(is_owner)
-
-        @pl.when(gathers)
-        def _():
-            land(0, pos)
-
-        @pl.when(jnp.logical_not(gathers))
-        def _():
-            from_sib(0, pos)
-
     def blk_at(pos):
         off = jnp.where(pos == 1, -s, jnp.where(pos == 2, s, jnp.where(pos == 3, 2, 0)))
         return ring(x + off)
@@ -470,24 +459,37 @@
         def _():
             from_owner(2)
 
+            @gatherer(True)
+            def _():
+                land(0, 2)
+
         @pl.when(step == 8)
         def _():
-            get_main(True, 2)
-
-        @pl.when(step == 9)
+            @gatherer(False)
+            def _():
+                from_sib(0, 2)
+
+        @pl.when(step == 11)
         def _():
             land_second(3)
+
+            @gatherer(False)
+            def _():
+                land(0, 3)
+
+        @pl.when(step == 12)
+        def _():
             from_owner(3)
 
-        @pl.when(step == 10)
-        def _():
-            get_main(False, 3)
+            @gatherer(True)
+            def _():
+                land(0, 3)
 
         @pl.when(step == 13)
         def _():
             @gatherer(True)
             def _():
-                land(0, 3)
+                from_sib(0, 3)
 
         @pl.when(step == 14)
         def _():
@@ -495,11 +497,11 @@
             def _():
                 from_sib(0, 3)
 
-        late_slot = jnp.where((step == 4) | (step == 5) | (step == 10), slot_a, 2)
+        late_slot = jnp.where((step == 4) | (step == 5) | (step == 13), slot_a, 2)
         slot = jnp.where(step < 3, step, jnp.where((step == 3) | (step == 8) | (step == 14), slot_b, late_slot))
         late_pos = jnp.where((step == 5) | (step == 6) | (step == 8), 2, 3)
         pos = jnp.where(step < 3, 0, jnp.where((step == 3) | (step == 4) | (step == 7), 1, late_pos))
-        summing = ((step >= 11) & (step < 14)) | (step == 15)
+        summing = ((step >= 9) & (step < 12)) | (step == 15)
 
         @pl.when(jnp.logical_not(summing))
         def _():
@@ -507,10 +509,10 @@
 
         @pl.when(summing)
         def _():
-            blk = blk_at(jnp.where(step == 15, 3, step - 11))
+            blk = blk_at(jnp.where(step == 15, 3, lax.rem(step + y, 3)))
             second_product(blk, 0, EARLY)
             send_rows(0, blk)
-            send_block(1, blk)
+            send_rows(1, blk)
 
     @pl.loop(0, 4)
     def _(pos):
@@ -528,8 +530,8 @@
     p2_end(1)
     x_send(XP)
     p2_end(2)
+    x_send(XO)
     p2_end(3)
-    x_send(XO)
     x_send(OWN)
 
     for d in range(1, 8):

time: 105 us -> 99.3 us (0.946)
  Pallas kernels: 103 us -> 97.4 us
    pallas_call x1, Pallas kernels: 103 us -> 97.4 us  [exchange(): pl.pallas_call(kernel, out_shape=jax.ShapeDtypeStruct((4, 40, BLK), F32),...]
where the time goes in v6:
time: 99.3 us; the launch traced here: 99.1 us
  Pallas kernels  97.4 us (98%)
  local copies, waits for them, and re-layouts  1.65 us (2%)
    pallas_call x1, Pallas kernels, exchange(): pl.pallas_call(kernel, out_shape=jax.ShapeDtypeStruct((4, 40, BLK), F32),...  97.4 us

profile of v6, /device:TPU:1, one launch (start us, length us, event | category | flops | bytes accessed | tf_op | source)
XLA Modules:
  0.0 99.1 jit_solution(2678521506047549157)
XLA Ops:
  0.0 97.4 %shard_map.64 = f32[4,40,320]{2,1,0:T(8,128)} custom-call(bf16[3,320,1280]{2,1,0:T(8,128)(2,1)} %b_in.1, bf16[10,4,1280]{2,1,0:T(4,128)(2,1)} %bitcast.7, bf16[3,160,1280]{2,1,0:T(8,128)(2,1)} %occ_in.1, s32[2,4]{1,0:T(2,128)} %bitcast.9, s32[80,20]{1,0:T(8,128)} %bitcast.8, s32[20,20]{1,0:T(8,128)} %i_tiles.1), custom_call_target="tpu_custom_call" | custom-call | tf_op jit(solution)/shard_map/pallas_call | solution.py:569
  97.5 1.7 %copy.8 = f32[4,320,40]{1,2,0:T(8,128)} copy(f32[4,320,40]{1,2,0:T(8,128)} %bitcast.6) | data formatting | bytes 409600

commit v7 on v6

--- a/solution.py
+++ b/solution.py
@@ -14,7 +14,7 @@
 HALF = 640
 EARLY = 768
 WIDE = 512
-PARTS = ((0, 0, WIDE), (0, WIDE, 256), (1, EARLY, 384), (0, EARLY + 384, 128))
+PARTS = ((0, 0, WIDE), (0, WIDE, 256), (1, EARLY, 256), (0, EARLY + 256, 256))
 OWN, XM, XP, XO = range(4)
 LAID = (
     ((640, 0, 128), (1088, 128, 192)),
@@ -337,6 +337,25 @@
     def width(n):
         return pl.ds(0, PARTS[n][2])
 
+    def early_copy(n, m, t):
+        at = (n, m, t, slice(None), width(n))
+        return rcopy(s1.at[at], r1.at[at], p1_ss.at[n, m, t], p1_rs.at[n, m, t],
+                     ralong(n, 0, (sg, -sg, sg)[m])[1])
+
+    def send_early(n, t):
+        for m, off in ((0, 2), (1, -sg)):
+            s1[n, m, t, :, width(n)] = part(n, t, ralong(n, 0, off)[0]).astype(BF16)
+            early_copy(n, m, t).start()
+
+    def pass_early(t):
+        for n in range(2):
+            early_copy(n, 0, t).wait_recv()
+            s1[n, 2, t, :, width(n)] = (part(n, t, ralong(n, 0, sg)[0]) + got1(n, 0, t)).astype(BF16)
+            early_copy(n, 2, t).start()
+
+    def early_blk(step):
+        return blk_at(jnp.where(step == 15, 3, lax.rem(step + y, 3)))
+
     def row_copy(n, m, t):
         at = (n, m, t, slice(None), width(n))
         return rcopy(s1.at[at], r1.at[at], p1_ss.at[n, m, t], p1_rs.at[n, m, t], ralong(n, 0, hops[m])[1])
@@ -358,9 +377,13 @@
                     s1[n, m, t, :, width(n)] = acc[blk, t, :, cols_of(n)].astype(BF16)
                 blk_copy(n, m).start()
 
-    def p1_each(n, what):
-        for m in range(3):
-            if PARTS[n][0] == 0:
+    def p1_each(n, what, first=0):
+        for m in range(first, 3):
+            if n < 2:
+                @pl.loop(0, 4)
+                def _(t):
+                    what(early_copy(n, m, t))
+            elif PARTS[n][0] == 0:
                 @pl.loop(0, 4)
                 def _(t):
                     what(row_copy(n, m, t))
@@ -372,9 +395,11 @@
 
     def p1_end(n):
         here = ralong(n, 0, 0)[0]
-        p1_each(n, lambda c: c.wait_recv())
+        p1_each(n, lambda c: c.wait_recv(), 1 if n < 2 else 0)
 
         def total(t):
+            if n < 2:
+                return part(n, t, here) + (got1(n, 1, t) + got1(n, 2, t))
             return (part(n, t, here) + got1(n, 0, t)) + (got1(n, 1, t) + got1(n, 2, t))
 
         for m in range(3):
@@ -477,6 +502,10 @@
             def _():
                 land(0, 3)
 
+        @pl.when((step >= 13) & (step < 16))
+        def _():
+            pass_early(early_blk(step - 4))
+
         @pl.when(step == 12)
         def _():
             from_owner(3)
@@ -509,10 +538,10 @@
 
         @pl.when(summing)
         def _():
-            blk = blk_at(jnp.where(step == 15, 3, lax.rem(step + y, 3)))
+            blk = early_blk(step)
             second_product(blk, 0, EARLY)
-            send_rows(0, blk)
-            send_rows(1, blk)
+            send_early(0, blk)
+            send_early(1, blk)
 
     @pl.loop(0, 4)
     def _(pos):
@@ -520,6 +549,11 @@
         second_product(blk, EARLY, V - EARLY)
         send_rows(3, blk)
         send_block(2, blk)
+
+        @pl.when(pos == 2)
+        def _():
+            pass_early(xo)
+
 
     p1_end(0)
     p1_end(1)
@@ -530,8 +564,8 @@
     p2_end(1)
     x_send(XP)
     p2_end(2)
+    p2_end(3)
     x_send(XO)
-    p2_end(3)
     x_send(OWN)
 
     for d in range(1, 8):

time: 99.3 us -> 97.7 us (0.984)
  Pallas kernels: 97.4 us -> 94.9 us
    pallas_call x1, Pallas kernels: 97.4 us -> 94.9 us  [exchange(): pl.pallas_call(kernel, out_shape=jax.ShapeDtypeStruct((4, 40, BLK), F32),...]
where the time goes in v7:
time: 97.7 us; the launch traced here: 96.5 us
  Pallas kernels  94.9 us (97%)
  local copies, waits for them, and re-layouts  1.65 us (2%)
    pallas_call x1, Pallas kernels, exchange(): pl.pallas_call(kernel, out_shape=jax.ShapeDtypeStruct((4, 40, BLK), F32),...  94.9 us

profile of v7, /device:TPU:1, one launch (start us, length us, event | category | flops | bytes accessed | tf_op | source)
XLA Modules:
  0.0 96.5 jit_solution(459962757572982809)
XLA Ops:
  0.0 94.9 %shard_map.64 = f32[4,40,320]{2,1,0:T(8,128)} custom-call(bf16[3,320,1280]{2,1,0:T(8,128)(2,1)} %b_in.1, bf16[10,4,1280]{2,1,0:T(4,128)(2,1)} %bitcast.7, bf16[3,160,1280]{2,1,0:T(8,128)(2,1)} %occ_in.1, s32[2,4]{1,0:T(2,128)} %bitcast.9, s32[80,20]{1,0:T(8,128)} %bitcast.8, s32[20,20]{1,0:T(8,128)} %i_tiles.1), custom_call_target="tpu_custom_call" | custom-call | tf_op jit(solution)/shard_map/pallas_call | solution.py:603
  94.9 1.7 %copy.8 = f32[4,320,40]{1,2,0:T(8,128)} copy(f32[4,320,40]{1,2,0:T(8,128)} %bitcast.6) | data formatting | bytes 409600

commit v8 on v7

--- a/solution.py
+++ b/solution.py
@@ -550,22 +550,22 @@
         send_rows(3, blk)
         send_block(2, blk)
 
-        @pl.when(pos == 2)
+        @pl.when(pos == 1)
         def _():
             pass_early(xo)
 
 
+    p1_end(2)
+    p1_end(3)
     p1_end(0)
     p1_end(1)
-    p1_end(2)
-    p1_end(3)
+    p2_end(2)
+    p2_end(3)
+    x_send(XO)
     p2_end(0)
     x_send(XM)
     p2_end(1)
     x_send(XP)
-    p2_end(2)
-    p2_end(3)
-    x_send(XO)
     x_send(OWN)
 
     for d in range(1, 8):

time: 97.7 us -> 97.4 us (level); the launches traced: 96.5 us -> 97.2 us
  no operation moved by 1% of the time
where the time goes in v8:
time: 97.4 us; the launch traced here: 97.2 us
  Pallas kernels  95.6 us (98%)
  local copies, waits for them, and re-layouts  1.65 us (2%)
    pallas_call x1, Pallas kernels, exchange(): pl.pallas_call(kernel, out_shape=jax.ShapeDtypeStruct((4, 40, BLK), F32),...  95.6 us

profile of v8, /device:TPU:1, one launch (start us, length us, event | category | flops | bytes accessed | tf_op | source)
XLA Modules:
  0.0 97.2 jit_solution(10864320626325067068)
XLA Ops:
  0.0 95.6 %shard_map.64 = f32[4,40,320]{2,1,0:T(8,128)} custom-call(bf16[3,320,1280]{2,1,0:T(8,128)(2,1)} %b_in.1, bf16[10,4,1280]{2,1,0:T(4,128)(2,1)} %bitcast.7, bf16[3,160,1280]{2,1,0:T(8,128)(2,1)} %occ_in.1, s32[2,4]{1,0:T(2,128)} %bitcast.9, s32[80,20]{1,0:T(8,128)} %bitcast.8, s32[20,20]{1,0:T(8,128)} %i_tiles.1), custom_call_target="tpu_custom_call" | custom-call | tf_op jit(solution)/shard_map/pallas_call | solution.py:603
  95.6 1.7 %copy.8 = f32[4,320,40]{1,2,0:T(8,128)} copy(f32[4,320,40]{1,2,0:T(8,128)} %bitcast.6) | data formatting | bytes 409600
